TPU v7x, 512 devices: a whole 4x8x8 slice. The times are simulated.
512 devices in a mesh: dom: 128 (over z, y, core), sub: 4 (over x).
Axes of the slice: x: 4, y: 8, z: 8, core: 2. Of those that a mesh axis runs over, the one named last changes fastest.
Arguments:
- positions: float32 [3, 1048576], P(None, ('dom', 'sub')), may hold values from -6 to 6
- fixed_mask: int32 [1048576], P(('dom', 'sub')), may hold values 0 or 1
- send_count: int32 [128, 4, 5, 4], P('dom', 'sub'), may hold values from 0 to 128, as said below
- send_list: int32 [128, 4, 5, 4, 128], P('dom', 'sub'), may hold values from 0 to 2047, as said below
- block_nodes: int32 [64, 65536], P(None, ('dom', 'sub')), may hold values from 0 to 4607, as said below
- tet_corners: int32 [4, 8388608], P(None, ('dom', 'sub')), may hold values from 0 to 63, as said below
Outputs:
- smoothed: float32 [3, 1048576], P(None, ('dom', 'sub'))
Inputs may be any that keep to these rules, and one draw needn't show every extreme that they name: send_count[d, s, k, t] is the number of nodes that partition (d, s) sends to the partition at dom index (d + k - 2) modulo the dom axis's size and sub index t; it is zero for k = 2, t = s. send_list[d, s, k, t, j] for j below send_count[d, s, k, t] is the local index of an owned node of partition (d, s), sent to that neighbour's ghost slot (k, s, j); later entries are ignored. `block_nodes`: entries are local columns of the block's partition: below 2048 an owned node, else 2048 + (k * 4 + t) * 128 + j for a ghost slot whose j is below the sending partition's count. `tet_corners`: the four corners of a tetrahedron are distinct rows.
All inputs are finite; a program needn't handle non-finite values. No bound on the sum of `fixed_mask` on one device may be relied on, other than what follows from the above.
Results may differ from a plain program's by a relative error of at most 0.0003.
Values sent between devices are 32-bit elements; how exact they have to be, the bound alone decides.
A program may use at most 128 MiB of HBM per device.

v0:
```python
import math

import jax
import jax.numpy as jnp
from jax import lax
from jax.sharding import PartitionSpec as P

ITERS = 2


delta_reg = 2.0
step_size = 0.01
winv_rows = (
    (1.0, -1.0 / math.sqrt(3.0), -1.0 / math.sqrt(6.0)),
    (0.0, 2.0 / math.sqrt(3.0), -1.0 / math.sqrt(6.0)),
    (0.0, 0.0, math.sqrt(1.5)),
)


def from_behind(value, axis, steps):
    count = lax.axis_size(axis)
    pairs = [(source, (source + steps) % count) for source in range(count)]
    return lax.ppermute(value, axis, pairs)


def distortion_sum(corners):
    edge_rows = [[corners[r, m + 1] - corners[r, 0] for m in range(3)] for r in range(3)]
    shape_mat = []
    for r in range(3):
        row_vals = []
        for c in range(3):
            acc_val = None
            for m in range(3):
                if winv_rows[m][c] != 0.0:
                    term_val = edge_rows[r][m] * winv_rows[m][c]
                    acc_val = term_val if acc_val is None else acc_val + term_val
            row_vals.append(acc_val)
        shape_mat.append(row_vals)
    norm_sq = shape_mat[0][0] * shape_mat[0][0]
    for r in range(3):
        for c in range(3):
            if r + c > 0:
                norm_sq = norm_sq + shape_mat[r][c] * shape_mat[r][c]
    volume_det = (
        shape_mat[0][0] * (shape_mat[1][1] * shape_mat[2][2] - shape_mat[1][2] * shape_mat[2][1])
        - shape_mat[0][1] * (shape_mat[1][0] * shape_mat[2][2] - shape_mat[1][2] * shape_mat[2][0])
        + shape_mat[0][2] * (shape_mat[1][0] * shape_mat[2][1] - shape_mat[1][1] * shape_mat[2][0])
    )
    root_term = jnp.sqrt(volume_det * volume_det + 4.0 * delta_reg * delta_reg)
    upper_part = 0.5 * (volume_det + root_term)
    lower_den = jnp.where(volume_det < 0, root_term - volume_det, 1.0)
    height = jnp.where(volume_det >= 0, upper_part, 2.0 * delta_reg * delta_reg / lower_den)
    distortion = norm_sq / (3.0 * height ** (2.0 / 3.0))
    return jnp.sum(distortion)


def tet_energy(local_nodes, block_nodes, tet_corners):
    block_count = block_nodes.shape[1]
    group_size = math.gcd(block_count, 16)
    group_count = block_count // group_size
    block_coords = local_nodes[:, block_nodes.T]
    block_coords = block_coords.reshape(3, group_count, group_size, 64).transpose(1, 0, 2, 3)
    corner_rows = tet_corners.reshape(4, group_count, group_size, 128).transpose(1, 0, 2, 3)
    column_ids = jnp.arange(64, dtype=jnp.int32)

    def group_energy(item):
        coords, rows = item
        incidence = (rows[:, :, :, None] == column_ids[None, None, None, :]).astype(jnp.float32)
        corners = jnp.einsum("rgm,ngim->rngi", coords, incidence, precision=lax.Precision.HIGHEST)
        return distortion_sum(corners)

    return jnp.sum(lax.map(group_energy, (block_coords, corner_rows)))


def offset_forward(payload, reach_doms):
    shifted = []
    for k in range(payload.shape[1]):
        offset = k - reach_doms
        if offset == 0:
            shifted.append(payload[:, k])
        else:
            shifted.append(from_behind(payload[:, k], "dom", offset))
    stacked = jnp.stack(shifted, axis=1)
    return lax.all_to_all(stacked, "sub", split_axis=2, concat_axis=2, tiled=True)


def offset_back(ghost_grad, reach_doms):
    moved = lax.all_to_all(ghost_grad, "sub", split_axis=2, concat_axis=2, tiled=True)
    shifted = []
    for k in range(moved.shape[1]):
        offset = k - reach_doms
        if offset == 0:
            shifted.append(moved[:, k])
        else:
            shifted.append(from_behind(moved[:, k], "dom", -offset))
    return jnp.stack(shifted, axis=1)


def per_device(positions, fixed_mask, send_count, send_list, block_nodes, tet_corners):
    node_count = positions.shape[1]
    slot_count = send_list.shape[2]
    sub_count = send_list.shape[3]
    slot_width = send_list.shape[4]
    reach_doms = (slot_count - 1) // 2
    counts = send_count[0, 0]
    send_rows = send_list[0, 0]
    slot_index = jnp.arange(slot_width, dtype=jnp.int32)
    valid_mask = slot_index[None, None, :] < counts[:, :, None]
    flat_rows = send_rows.reshape(-1)
    free_nodes = (fixed_mask == 0).astype(jnp.float32)
    grad_fn = jax.grad(tet_energy)
    owned_pos = positions
    for step in range(ITERS):
        picked = owned_pos[:, send_rows]
        payload = jnp.where(valid_mask[None], picked, 0.0)
        ghosts = offset_forward(payload, reach_doms)
        local_nodes = jnp.concatenate([owned_pos, ghosts.reshape(3, -1)], axis=1)
        local_grad = grad_fn(local_nodes, block_nodes, tet_corners)
        ghost_grad = local_grad[:, node_count:].reshape(3, slot_count, sub_count, slot_width)
        returned = offset_back(ghost_grad, reach_doms)
        returned = jnp.where(valid_mask[None], returned, 0.0)
        grad_total = local_grad[:, :node_count].at[:, flat_rows].add(returned.reshape(3, -1))
        owned_pos = owned_pos - step_size * free_nodes[None, :] * grad_total
    return owned_pos


def solution(mesh):
    return jax.shard_map(
        per_device,
        mesh=mesh,
        in_specs=(
            P(None, ("dom", "sub")),
            P(("dom", "sub")),
            P("dom", "sub", None, None),
            P("dom", "sub", None, None, None),
            P(None, ("dom", "sub")),
            P(None, ("dom", "sub")),
        ),
        out_specs=P(None, ("dom", "sub")),
        check_vma=False,
    )
```

profile of v0, /device:TPU:1, one launch (start us, length us, event | category | flops | bytes accessed | tf_op | source)
XLA Modules:
  0.0 614.7 jit_solution(6712654509107781962)
XLA Ops:
  2.8 4.1 gather_fusion
  7.4 14.4 %collective-permute-start = (f32[3,4,128]{2,0,1:T(4,128)S(1)}, f32[3,4,128]{2,0,1:T(4,128)S(1)}, u32[]{:S(2)}, u32[]{:S(2)}) collective-permute-start(f32[3,4,128]{2,0,1:T(4,128)S(1)} %get-tuple-element.2623), channel_id=1, source_target_pairs={{0,504},{4,508},{8,0},{12,4},{16,8},{20,12},{24,16},{28,20},{32,24... | collective-permute-start | bytes 18440 | tf_op jit(solution)/shard_map/ppermute | solution.py:23
  35.6 4.0 all-to-all-start
  39.7 4.3 all-to-all-done
  44.8 27.9 %gather_fusion.1 = f32[8192,3]{1,0:T(8,128)} fusion(f32[3,4608]{0,1:T(8,128)S(1)} %copy.365, s32[8192]{0:T(1024)S(1)} %broadcast_clamp_fusion), kind=kCustom, calls=%fused_computation.1 | custom fusion | bytes 229376 | tf_op jit(solution)/shard_map/jvp()/gather | solution.py:61
  75.7 7.9 %broadcast.6173.clone2 = f32[8,4,16,128,64]{3,4,1,2,0:T(8,128)} broadcast(f32[]{:T(128)} %constant.454.clone.1), dimensions={} | broadcast | bytes 16777220 | tf_op jit(solution)/shard_map/broadcast.99
  90.6 90.4 %while.140 = (s32[]{:T(128)}, f32[8,4,16,128,64]{3,4,1,2,0:T(8,128)}, f32[8,16,128]{2,1,0:T(8,128)S(1)}, f32[8,16,128]{2,1,0:T(8,128)S(1)}, f32[8,16,128]{2,1,0:...) while((s32[]{:T(128)}, ...), condition=%wide.region_1.2_spmd.clone.clone, body=%wide.region_0.1_spmd.clone.clone.sunk | while | flops 20658176 | bytes 11525365 | solution.py:72
  181.8 46.4 %while.138 = (s32[]{:T(128)}, f32[8,3,16,64]{3,1,2,0:T(4,128)S(1)}, f32[8,16,128]{2,1,0:T(8,128)S(1)}, f32[8,16,128]{2,1,0:T(8,128)S(1)}, pred[8,16,128]{2,1,0:T...) while((s32[]{:T(128)}, f32[8,3,16,64]{3,1,2,0:T(4,128)S(1)}, ...), condition=%wide.region_3.4_spmd, body=%wide.region_2.3_spmd.sunk | while | flops 19525636 | bytes 3093761 | solution.py:72
  184.1 3.4 fusion.155
  189.9 3.4 fusion.155
  195.7 3.4 fusion.155
  207.3 3.4 fusion.155
  230.9 44.9 %scatter_custom_fusion = f32[3,4608]{0,1:T(8,128)S(1)} fusion(s32[8192]{0:T(1024)S(1)} %reshape.10082, f32[8192,3]{1,0:T(8,128)} %bitcast.726, f32[]{:T(128)} %constant.454.clone.1), kind=kCustom, calls=%fused_computation.293 | custom fusion | flops 24576 | bytes 55808 | tf_op jit(solution)/shard_map/transpose(jvp())/scatter-add | solution.py:61
  282.8 4.3 all-to-all-done.1
  291.6 5.0 collective-permute-start.6
  296.5 7.0 %collective-permute-start.7 = (f32[3,4,128]{2,0,1:T(4,128)S(1)}, f32[3,4,128]{2,0,1:T(4,128)S(1)}, u32[]{:S(2)}, u32[]{:S(2)}) collective-permute-start(f32[3,4,128]{2,0,1:T(4,128)S(1)} %get-tuple-element.2615), channel_id=1, source_target_pairs={{0,504},{4,508},{8,0},{12,4},{16,8},{20,12},{24,16},{28,20},{32,24... | collective-permute-start | bytes 18440 | tf_op jit(solution)/shard_map/ppermute | solution.py:23
  308.3 14.8 %scatter_custom_fusion.1 = f32[3,2048]{0,1:T(8,128)S(1)} fusion(f32[3,2048]{0,1:T(8,128)S(1)} %slice-done, s32[2560]{0:T(1024)S(1)} %fusion.98, f32[3,2560]{0,1:T(8,128)S(1)} %bitcast_select_fusion.1), kind=kCustom, calls=%fused_computation.288 | custom fusion | flops 7680 | bytes 1335296 | tf_op jit(solution)/shard_map/scatter-add | solution.py:122
  323.8 4.1 gather_fusion.2
  328.4 6.9 %collective-permute-start.8 = (f32[3,4,128]{2,0,1:T(4,128)S(1)}, f32[3,4,128]{2,0,1:T(4,128)S(1)}, u32[]{:S(2)}, u32[]{:S(2)}) collective-permute-start(f32[3,4,128]{2,0,1:T(4,128)S(1)} %get-tuple-element.2614), channel_id=1, source_target_pairs={{0,504},{4,508},{8,0},{12,4},{16,8},{20,12},{24,16},{28,20},{32,24... | collective-permute-start | bytes 18440 | tf_op jit(solution)/shard_map/ppermute | solution.py:23
  335.4 5.1 collective-permute-start.9
  345.1 6.2 %collective-permute-done.11 = f32[3,4,128]{2,0,1:T(4,128)S(1)} collective-permute-done((f32[3,4,128]{2,0,1:T(4,128)S(1)}, f32[3,4,128]{2,0,1:T(4,128)S(1)}, u32[]{:S(2)}, u32[]{:S(2)}) %collective-permute-start.11) | collective-permute-done | bytes 6176 | tf_op jit(solution)/shard_map/ppermute | solution.py:23
  355.3 4.3 all-to-all-done.2
  362.6 27.9 %gather_fusion.3 = f32[8192,3]{1,0:T(8,128)} fusion(f32[3,4608]{0,1:T(8,128)S(1)} %pad_maximum_fusion, s32[8192]{0:T(1024)S(1)} %broadcast_clamp_fusion), kind=kCustom, calls=%fused_computation.3 | custom fusion | bytes 229376 | tf_op jit(solution)/shard_map/jvp()/gather | solution.py:61
  393.5 7.9 %broadcast.6173.clone = f32[8,4,16,128,64]{3,4,1,2,0:T(8,128)} broadcast(f32[]{:T(128)} %constant.454.clone.1), dimensions={} | broadcast | bytes 16777220 | tf_op jit(solution)/shard_map/broadcast.99
  402.9 82.8 %while.141 = (s32[]{:T(128)}, f32[8,4,16,128,64]{3,4,1,2,0:T(8,128)}, f32[8,16,128]{2,1,0:T(8,128)S(1)}, f32[8,16,128]{2,1,0:T(8,128)S(1)}, f32[8,16,128]{2,1,0:...) while((s32[]{:T(128)}, ...), condition=%wide.region_7.8_spmd.clone.clone, body=%wide.region_6.7_spmd.clone.clone.sunk | while | flops 20658176 | bytes 11523841 | solution.py:72
  485.8 34.6 %while.139 = (s32[]{:T(128)}, f32[8,3,16,64]{3,1,2,0:T(4,128)S(1)}, f32[8,16,128]{2,1,0:T(8,128)S(1)}, f32[8,16,128]{2,1,0:T(8,128)S(1)}, pred[8,16,128]{2,1,0:T...) while((s32[]{:T(128)}, f32[8,3,16,64]{3,1,2,0:T(4,128)S(1)}, ...), condition=%wide.region_9.10_spmd, body=%wide.region_8.9_spmd.sunk | while | flops 19525636 | bytes 3093761 | solution.py:72
  508.3 3.4 fusion.162
  523.1 44.9 %scatter_custom_fusion.2 = f32[3,4608]{0,1:T(8,128)S(1)} fusion(s32[8192]{0:T(1024)} %copy-done.5, f32[8192,3]{1,0:T(8,128)} %bitcast.725, f32[]{:T(128)} %constant.454.clone.1), kind=kCustom, calls=%fused_computation.291 | custom fusion | flops 24576 | bytes 55808 | tf_op jit(solution)/shard_map/transpose(jvp())/scatter-add | solution.py:61
  571.0 6.7 %all_to_all.20 = f32[3,5,4,128]{3,0,1,2:T(4,128)S(1)} all-to-all(f32[3,5,4,128]{3,0,1,2:T(4,128)S(1)} %copy.388), channel_id=1, replica_groups=mesh['dom'=128,'sub'=4] {'sub'}, dimensions={2} | all-to-all | bytes 61440 | tf_op jit(solution)/shard_map/all_to_all | solution.py:88
  581.7 5.6 collective-permute-start.14
  587.3 7.2 %collective-permute-start.15 = (f32[3,4,128]{2,0,1:T(4,128)S(1)}, f32[3,4,128]{2,0,1:T(4,128)S(1)}, u32[]{:S(2)}, u32[]{:S(2)}) collective-permute-start(f32[3,4,128]{2,0,1:T(4,128)S(1)} %get-tuple-element.2605), channel_id=1, source_target_pairs={{0,504},{4,508},{8,0},{12,4},{16,8},{20,12},{24,16},{28,20},{32,24... | collective-permute-start | bytes 18440 | tf_op jit(solution)/shard_map/ppermute | solution.py:23
  599.0 14.8 %scatter_custom_fusion.3 = f32[3,2048]{0,1:T(8,128)S(1)} fusion(f32[3,2048]{0,1:T(8,128)S(1)} %slice-done.1, s32[2560]{0:T(1024)} %copy-done.12, f32[3,2560]{0,1:T(8,128)S(1)} %bitcast_select_fusion), kind=kCustom, calls=%fused_computation.285 | custom fusion | flops 7680 | bytes 1335296 | tf_op jit(solution)/shard_map/scatter-add | solution.py:122
  (484 shorter events, 315.4 us)
Async XLA Ops:
  0.0 44.0 %copy-start.3 = (f32[3,2048]{1,0:T(4,128)S(1)}, f32[3,2048]{1,0:T(4,128)}, u32[]{:S(2)}) copy-start(f32[3,2048]{1,0:T(4,128)} %param.14) | copy-start | bytes 73732
  0.0 29.3 %copy-start.9 = (s32[64,128]{1,0:T(8,128)S(1)}, s32[64,128]{1,0:T(8,128)}, u32[]{:S(2)}) copy-start(s32[64,128]{1,0:T(8,128)} %param.18) | copy-start | bytes 98308
  0.0 39.7 %copy-start.4 = (s32[4,16384]{1,0:T(4,128)S(1)}, s32[4,16384]{1,0:T(4,128)}, u32[]{:S(2)}) copy-start(s32[4,16384]{1,0:T(4,128)} %param.19) | copy-start | bytes 786436
  7.4 22.1 %collective-permute-start = (f32[3,4,128]{2,0,1:T(4,128)S(1)}, f32[3,4,128]{2,0,1:T(4,128)S(1)}, u32[]{:S(2)}, u32[]{:S(2)}) collective-permute-start(f32[3,4,128]{2,0,1:T(4,128)S(1)} %get-tuple-element.2623), channel_id=1, source_target_pairs={{0,504},{4,508},{8,0},{12,4},{16,8},{20,12},{24,16},{28,20},{32,24... | collective-permute-start | bytes 18440 | tf_op jit(solution)/shard_map/ppermute | solution.py:23
  21.8 8.3 %collective-permute-start.1 = (f32[3,4,128]{2,0,1:T(4,128)S(1)}, f32[3,4,128]{2,0,1:T(4,128)S(1)}, u32[]{:S(2)}, u32[]{:S(2)}) collective-permute-start(f32[3,4,128]{2,0,1:T(4,128)S(1)} %get-tuple-element.2622), channel_id=1, source_target_pairs={{0,508},{4,0},{8,4},{12,8},{16,12},{20,16},{24,20},{28,24},{32,28}... | collective-permute-start | bytes 18440 | tf_op jit(solution)/shard_map/ppermute | solution.py:23
  24.6 6.6 %collective-permute-start.2 = (f32[3,4,128]{2,0,1:T(4,128)S(1)}, f32[3,4,128]{2,0,1:T(4,128)S(1)}, u32[]{:S(2)}, u32[]{:S(2)}) collective-permute-start(f32[3,4,128]{2,0,1:T(4,128)S(1)} %get-tuple-element.2621), channel_id=1, source_target_pairs={{0,4},{4,8},{8,12},{12,16},{16,20},{20,24},{24,28},{28,32},{32,36}... | collective-permute-start | bytes 18440 | tf_op jit(solution)/shard_map/ppermute | solution.py:23
  27.3 7.7 %collective-permute-start.3 = (f32[3,4,128]{2,0,1:T(4,128)S(1)}, f32[3,4,128]{2,0,1:T(4,128)S(1)}, u32[]{:S(2)}, u32[]{:S(2)}) collective-permute-start(f32[3,4,128]{2,0,1:T(4,128)S(1)} %get-tuple-element.2620), channel_id=1, source_target_pairs={{0,8},{4,12},{8,16},{12,20},{16,24},{20,28},{24,32},{28,36},{32,40... | collective-permute-start | bytes 18440 | tf_op jit(solution)/shard_map/ppermute | solution.py:23
  29.5 201.5 %copy-start.5 = (s32[8192]{0:T(1024)}, s32[8192]{0:T(1024)S(1)}, u32[]{:S(2)}) copy-start(s32[8192]{0:T(1024)S(1)} %reshape.10082) | copy-start | bytes 98308
  35.6 8.4 %all-to-all-start = ((f32[3,5,4,128]{3,0,1,2:T(4,128)}), f32[3,5,4,128]{3,0,1,2:T(4,128)S(1)}, u32[]{:S(2)}, u32[]{:S(2)}) async-start(f32[3,5,4,128]{3,0,1,2:T(4,128)} %constant_dynamic-update-slice_fusion.30), calls=%async_computation | async-start | bytes 81920 | tf_op jit(solution)/shard_map/all_to_all | solution.py:84
  275.8 13.2 %copy-start = (f32[3,4608]{0,1:T(8,128)}, f32[3,4608]{0,1:T(8,128)S(1)}, u32[]{:S(2)}) copy-start(f32[3,4608]{0,1:T(8,128)S(1)} %scatter_custom_fusion) | copy-start | bytes 165892
  275.9 13.1 %copy-start.8 = (s32[1,1,5,4,128]{4,3,2,1,0:T(4,128)S(1)}, s32[1,1,5,4,128]{4,3,2,1,0:T(4,128)}, u32[]{:S(2)}) copy-start(s32[1,1,5,4,128]{4,3,2,1,0:T(4,128)} %param.17) | copy-start | bytes 30724
  279.5 7.6 %all-to-all-start.1 = ((f32[3,5,4,128]{3,0,1,2:T(4,128)}), f32[3,5,4,128]{3,0,1,2:T(4,128)S(1)}, u32[]{:S(2)}, u32[]{:S(2)}) async-start(f32[3,5,4,128]{3,0,1,2:T(4,128)} %copy.370), calls=%async_computation.1 | async-start | bytes 81920 | tf_op jit(solution)/shard_map/all_to_all | solution.py:88
  282.8 40.7 %copy-start.6 = (f32[2048]{0:T(1024)}, f32[2048]{0:T(1024)S(1)}, u32[]{:S(2)}) copy-start(f32[2048]{0:T(1024)S(1)} %compare_select_fusion.3) | copy-start | bytes 24580
  287.1 16.4 %collective-permute-start.4 = (f32[3,4,128]{2,0,1:T(4,128)S(1)}, f32[3,4,128]{2,0,1:T(4,128)S(1)}, u32[]{:S(2)}, u32[]{:S(2)}) collective-permute-start(f32[3,4,128]{2,0,1:T(4,128)S(1)} %get-tuple-element.2619), channel_id=1, source_target_pairs={{0,8},{4,12},{8,16},{12,20},{16,24},{20,28},{24,32},{28,36},{32,40... | collective-permute-start | bytes 18440 | tf_op jit(solution)/shard_map/ppermute | solution.py:23
  289.0 19.2 %copy-start.12 = (s32[2560]{0:T(1024)}, s32[2560]{0:T(1024)S(1)}, u32[]{:S(2)}) copy-start(s32[2560]{0:T(1024)S(1)} %fusion.98) | copy-start | bytes 30724
  289.1 19.2 %copy-start.10 = (pred[2560]{0:T(1024)(128)(4,1)}, pred[2560]{0:T(1024)(128)(4,1)S(1)}, u32[]{:S(2)}) copy-start(pred[2560]{0:T(1024)(128)(4,1)S(1)} %lt.150) | copy-start | bytes 7684
  289.1 19.2 %slice-start = ((f32[3,4608]{0,1:T(8,128)}), f32[3,2048]{0,1:T(8,128)S(1)}, s32[]{:S(2)}) async-start(f32[3,4608]{0,1:T(8,128)} %copy-done), calls=%async_computation.4 | async-start | bytes 2097152 | tf_op jit(solution)/shard_map/slice | solution.py:122
  289.1 14.4 %collective-permute-start.5 = (f32[3,4,128]{2,0,1:T(4,128)S(1)}, f32[3,4,128]{2,0,1:T(4,128)S(1)}, u32[]{:S(2)}, u32[]{:S(2)}) collective-permute-start(f32[3,4,128]{2,0,1:T(4,128)S(1)} %get-tuple-element.2618), channel_id=1, source_target_pairs={{0,4},{4,8},{8,12},{12,16},{16,20},{20,24},{24,28},{28,32},{32,36}... | collective-permute-start | bytes 18440 | tf_op jit(solution)/shard_map/ppermute | solution.py:23
  291.6 12.0 %collective-permute-start.6 = (f32[3,4,128]{2,0,1:T(4,128)S(1)}, f32[3,4,128]{2,0,1:T(4,128)S(1)}, u32[]{:S(2)}, u32[]{:S(2)}) collective-permute-start(f32[3,4,128]{2,0,1:T(4,128)S(1)} %get-tuple-element.2616), channel_id=1, source_target_pairs={{0,508},{4,0},{8,4},{12,8},{16,12},{20,16},{24,20},{28,24},{32,28}... | collective-permute-start | bytes 18440 | tf_op jit(solution)/shard_map/ppermute | solution.py:23
  296.5 7.7 %collective-permute-start.7 = (f32[3,4,128]{2,0,1:T(4,128)S(1)}, f32[3,4,128]{2,0,1:T(4,128)S(1)}, u32[]{:S(2)}, u32[]{:S(2)}) collective-permute-start(f32[3,4,128]{2,0,1:T(4,128)S(1)} %get-tuple-element.2615), channel_id=1, source_target_pairs={{0,504},{4,508},{8,0},{12,4},{16,8},{20,12},{24,16},{28,20},{32,24... | collective-permute-start | bytes 18440 | tf_op jit(solution)/shard_map/ppermute | solution.py:23
  328.4 12.0 %collective-permute-start.8 = (f32[3,4,128]{2,0,1:T(4,128)S(1)}, f32[3,4,128]{2,0,1:T(4,128)S(1)}, u32[]{:S(2)}, u32[]{:S(2)}) collective-permute-start(f32[3,4,128]{2,0,1:T(4,128)S(1)} %get-tuple-element.2614), channel_id=1, source_target_pairs={{0,504},{4,508},{8,0},{12,4},{16,8},{20,12},{24,16},{28,20},{32,24... | collective-permute-start | bytes 18440 | tf_op jit(solution)/shard_map/ppermute | solution.py:23
  335.4 5.9 collective-permute-start.9
  341.3 3.9 collective-permute-start.10
  343.2 8.2 %collective-permute-start.11 = (f32[3,4,128]{2,0,1:T(4,128)S(1)}, f32[3,4,128]{2,0,1:T(4,128)S(1)}, u32[]{:S(2)}, u32[]{:S(2)}) collective-permute-start(f32[3,4,128]{2,0,1:T(4,128)S(1)} %get-tuple-element.2610), channel_id=1, source_target_pairs={{0,8},{4,12},{8,16},{12,20},{16,24},{20,28},{24,32},{28,36},{32,40... | collective-permute-start | bytes 18440 | tf_op jit(solution)/shard_map/ppermute | solution.py:23
  352.0 7.6 %all-to-all-start.2 = ((f32[3,5,4,128]{3,0,1,2:T(4,128)}), f32[3,5,4,128]{3,0,1,2:T(4,128)S(1)}, u32[]{:S(2)}, u32[]{:S(2)}) async-start(f32[3,5,4,128]{3,0,1,2:T(4,128)} %copy.380), calls=%async_computation.2 | async-start | bytes 81920 | tf_op jit(solution)/shard_map/all_to_all | solution.py:84
  569.3 27.3 %copy-start.11 = (pred[2560]{0:T(1024)(128)(4,1)S(1)}, pred[2560]{0:T(1024)(128)(4,1)}, u32[]{:S(2)}) copy-start(pred[2560]{0:T(1024)(128)(4,1)} %copy-done.10) | copy-start | bytes 7684
  577.7 16.8 %collective-permute-start.12 = (f32[3,4,128]{2,0,1:T(4,128)S(1)}, f32[3,4,128]{2,0,1:T(4,128)S(1)}, u32[]{:S(2)}, u32[]{:S(2)}) collective-permute-start(f32[3,4,128]{2,0,1:T(4,128)S(1)} %get-tuple-element.2609), channel_id=1, source_target_pairs={{0,8},{4,12},{8,16},{12,20},{16,24},{20,28},{24,32},{28,36},{32,40... | collective-permute-start | bytes 18440 | tf_op jit(solution)/shard_map/ppermute | solution.py:23
  579.6 19.3 %slice-start.1 = ((f32[3,4608]{0,1:T(8,128)}), f32[3,2048]{0,1:T(8,128)S(1)}, s32[]{:S(2)}) async-start(f32[3,4608]{0,1:T(8,128)} %copy-done.1), calls=%async_computation.5 | async-start | bytes 2097152 | tf_op jit(solution)/shard_map/slice | solution.py:122
  579.6 14.8 %collective-permute-start.13 = (f32[3,4,128]{2,0,1:T(4,128)S(1)}, f32[3,4,128]{2,0,1:T(4,128)S(1)}, u32[]{:S(2)}, u32[]{:S(2)}) collective-permute-start(f32[3,4,128]{2,0,1:T(4,128)S(1)} %get-tuple-element.2608), channel_id=1, source_target_pairs={{0,4},{4,8},{8,12},{12,16},{16,20},{20,24},{24,28},{28,32},{32,36}... | collective-permute-start | bytes 18440 | tf_op jit(solution)/shard_map/ppermute | solution.py:23
  581.7 12.8 %collective-permute-start.14 = (f32[3,4,128]{2,0,1:T(4,128)S(1)}, f32[3,4,128]{2,0,1:T(4,128)S(1)}, u32[]{:S(2)}, u32[]{:S(2)}) collective-permute-start(f32[3,4,128]{2,0,1:T(4,128)S(1)} %get-tuple-element.2606), channel_id=1, source_target_pairs={{0,508},{4,0},{8,4},{12,8},{16,12},{20,16},{24,20},{28,24},{32,28}... | collective-permute-start | bytes 18440 | tf_op jit(solution)/shard_map/ppermute | solution.py:23
  587.3 7.7 %collective-permute-start.15 = (f32[3,4,128]{2,0,1:T(4,128)S(1)}, f32[3,4,128]{2,0,1:T(4,128)S(1)}, u32[]{:S(2)}, u32[]{:S(2)}) collective-permute-start(f32[3,4,128]{2,0,1:T(4,128)S(1)} %get-tuple-element.2605), channel_id=1, source_target_pairs={{0,504},{4,508},{8,0},{12,4},{16,8},{20,12},{24,16},{28,20},{32,24... | collective-permute-start | bytes 18440 | tf_op jit(solution)/shard_map/ppermute | solution.py:23
  599.0 15.1 %copy-start.7 = (f32[2048]{0:T(1024)S(1)}, f32[2048]{0:T(1024)}, u32[]{:S(2)}) copy-start(f32[2048]{0:T(1024)} %copy-done.6) | copy-start | bytes 24580
  (3 other events, 19.2 us)
where the time goes:
time: 619 us; the launch traced here: 615 us
  other arithmetic  232 us (37%)
  local copies, waits for them, and re-layouts  201 us (32%)
  starting transfers between devices  81.3 us (13%)
  matrix products  67.2 us (11%)
  waiting for transfers between devices  24.2 us (4%)
  blocking collectives  6.7 us (1%)
    scatter-add x2, other arithmetic, tet_energy(): block_coords = local_nodes[:, block_nodes.T]  89.8 us
    dynamic_update_slice x80, local copies, waits for them, and re-layouts, tet_energy(): return jnp.sum(lax.map(group_energy, (block_coords, corner_rows)))  74.2 us
    ppermute x16, starting transfers between devices, from_behind(): return lax.ppermute(value, axis, pairs)  70.7 us
    dot_general x32, matrix products, group_energy(): jnp.einsum('rgm,ngim->rngi', coords, incidence, precision=lax.Precision.H...  67.2 us
    gather x4, local copies, waits for them, and re-layouts, tet_energy(): block_coords = local_nodes[:, block_nodes.T]  61.8 us
    convert_element_type x16, other arithmetic, group_energy(): (rows[:, :, :, None] == column_ids[None, None, None, :]).astype(jnp.float32)  48.5 us
    dynamic_update_slice x64, other arithmetic, tet_energy(): return jnp.sum(lax.map(group_energy, (block_coords, corner_rows)))  30.8 us
    scatter-add x2, other arithmetic, per_device(): local_grad[:, :node_count].at[:, flat_rows].add(returned.reshape(3, -1))  29.6 us
  transfers between devices with their start and end apart: 19, of which 8 were waited for; matrix products, arithmetic and copies ran while one was open for 0% of the time, Pallas kernels for 0%

commit v1 on v0

v1 whole, which is shorter than its diff:
```python
import functools
import math

import jax
import jax.numpy as jnp
from jax import lax
from jax.experimental import pallas as pl
from jax.experimental.pallas import tpu as pltpu
from jax.sharding import PartitionSpec as P

ITERS = 2
STEP = 0.01
DELTA = 2.0
REACH = 2
SLOTS = 5
SUBS = 4
NPAIR = SLOTS * SUBS
OWN_ROWS = 16
ROWS = OWN_ROWS + NPAIR
HPAD = 40
MESH = pl.DeviceIdType.MESH


def nt_dot(a, b):
    return lax.dot_general(a, b, (((1,), (1,)), ((), ())), preferred_element_type=jnp.float32)


def split_rows(x):
    low = x - x.astype(jnp.bfloat16).astype(jnp.float32)
    return jnp.concatenate([x, low], axis=0).astype(jnp.bfloat16)


def lane_take(row, lanes):
    src = jnp.broadcast_to(row, lanes.shape)
    return jnp.take_along_axis(src, lanes, axis=1, mode="promise_in_bounds")


def send_columns(list_ref, count_ref, cols_ref):
    lane = lax.broadcasted_iota(jnp.int32, (1, 128), 1)
    for k in range(SLOTS):
        for t in range(SUBS):
            row = list_ref[0, 0, k, t : t + 1, :]
            cols_ref[k * SUBS + t : k * SUBS + t + 1, :] = jnp.where(lane < count_ref[0, 0, k, t], row, -1)


def gather_payload(pos_ref, cols_ref, pay_ref):
    cols = jnp.concatenate([cols_ref[...], jnp.full((24 - NPAIR, 128), -1, jnp.int32)], axis=0)
    high = cols >> 7
    low = cols & 127
    for r in range(3):
        acc = jnp.zeros((24, 128), jnp.float32)
        for h in range(OWN_ROWS):
            picked = lane_take(pos_ref[r * OWN_ROWS + h : r * OWN_ROWS + h + 1, :], low)
            acc = jnp.where(high == h, picked, acc)
        for n in range(NPAIR):
            pay_ref[n, r : r + 1, :] = acc[n : n + 1, :]
    for n in range(NPAIR):
        pay_ref[n, 3:4, :] = jnp.zeros((1, 128), jnp.float32)


def tet_gradient(corner):
    edge = [[corner[m + 1][r] - corner[0][r] for r in range(3)] for m in range(3)]
    total = [edge[0][r] + edge[1][r] + edge[2][r] for r in range(3)]
    squares = None
    for m in range(3):
        for r in range(3):
            term = edge[m][r] * edge[m][r]
            squares = term if squares is None else squares + term
    spread = total[0] * total[0] + total[1] * total[1] + total[2] * total[2]
    norm_sq = 2.0 * squares - 0.5 * spread

    def cross(a, b):
        return [
            a[1] * b[2] - a[2] * b[1],
            a[2] * b[0] - a[0] * b[2],
            a[0] * b[1] - a[1] * b[0],
        ]

    cof = [cross(edge[1], edge[2]), cross(edge[2], edge[0]), cross(edge[0], edge[1])]
    root2 = math.sqrt(2.0)
    det = root2 * (edge[0][0] * cof[0][0] + edge[0][1] * cof[0][1] + edge[0][2] * cof[0][2])
    root = jnp.sqrt(det * det + 4.0 * DELTA * DELTA)
    far = root + jnp.abs(det)
    height = jnp.where(det >= 0, 0.5 * far, (2.0 * DELTA * DELTA) / far)
    factor = (2.0 / 3.0) * jnp.exp((-2.0 / 3.0) * jnp.log(height))
    pull = (root2 / 3.0) * norm_sq / root
    grads = []
    for m in range(3):
        grads.append([factor * (2.0 * edge[m][r] - 0.5 * total[r] - pull * cof[m][r]) for r in range(3)])
    first = [-(grads[0][r] + grads[1][r] + grads[2][r]) for r in range(3)]
    return [first] + grads


def prepare_blocks(nodes_ref, packed_ref):
    turned = nodes_ref[...].T
    packed_ref[...] = jnp.concatenate([turned[0:64, :], turned[64:128, :]], axis=1)


def local_gradient(pos_ref, ghost_ref, packed_ref, corners_ref, spread_ref, acc_ref):
    acc_ref[...] = jnp.zeros_like(acc_ref)

    def body(j, carry):
        base = pl.multiple_of(j * 8, 8)
        cols = packed_ref[pl.ds(base, 8), :]
        high = cols >> 7
        low = cols & 127
        source = []
        for r in range(3):
            picked = jnp.zeros((8, 128), jnp.float32)
            for h in range(ROWS):
                if h < OWN_ROWS:
                    row = pos_ref[r * OWN_ROWS + h : r * OWN_ROWS + h + 1, :]
                else:
                    row = ghost_ref[h - OWN_ROWS, r : r + 1, :]
                picked = jnp.where(high == h, lane_take(row, low), picked)
            source.append(picked)
        for half in range(2):
            block = half * 64 + base
            corner = []
            for c in range(4):
                lanes = corners_ref[pl.ds(block * 4 + c, 8, stride=4), :] + 64 * half
                corner.append([jnp.take_along_axis(source[r], lanes, axis=1, mode="promise_in_bounds") for r in range(3)])
            grads = tet_gradient(corner)
            for c in range(4):
                for r in range(3):
                    start = (c * 3 + r) * 16 + half * 8
                    spread_ref[start : start + 8, :] = grads[c][r]
        node_iota = lax.broadcasted_iota(jnp.int32, (64, 128), 0)
        high_iota = lax.broadcasted_iota(jnp.int32, (HPAD, 128), 0)
        low_iota = lax.broadcasted_iota(jnp.int32, (128, 128), 0)
        left_parts = []
        right_parts = []
        for i in range(8):
            sums = []
            for half in range(2):
                parts = []
                marks = []
                for c in range(4):
                    rows = spread_ref[pl.ds(c * 48 + half * 8 + i, 8, stride=16), :]
                    parts.append(split_rows(rows))
                    ids = corners_ref[pl.ds((half * 64 + base + i) * 4 + c, 1), :]
                    marks.append(jnp.where(node_iota == ids, 1.0, 0.0).astype(jnp.bfloat16))
                out = nt_dot(jnp.concatenate(parts, axis=1), jnp.concatenate(marks, axis=1))
                sums.append(out[0:8, :] + out[8:16, :])
            pair = jnp.concatenate(sums, axis=1)
            pair_low = pair - pair.astype(jnp.bfloat16).astype(jnp.float32)
            chosen = high_iota == high[i : i + 1, :]
            stack = [jnp.where(chosen, pair[r : r + 1, :], 0.0) for r in range(3)]
            stack += [jnp.where(chosen, pair_low[r : r + 1, :], 0.0) for r in range(3)]
            left_parts.append(jnp.concatenate(stack, axis=0).astype(jnp.bfloat16))
            right_parts.append(jnp.where(low_iota == low[i : i + 1, :], 1.0, 0.0).astype(jnp.bfloat16))
        acc_ref[...] += nt_dot(jnp.concatenate(left_parts, axis=1), jnp.concatenate(right_parts, axis=1))
        return carry

    lax.fori_loop(0, 8, body, 0)


def put_gradient(acc_ref, own_ref, out_ref):
    for r in range(3):
        both = acc_ref[r * HPAD : (r + 1) * HPAD, :] + acc_ref[(3 + r) * HPAD : (4 + r) * HPAD, :]
        own_ref[r * OWN_ROWS : (r + 1) * OWN_ROWS, :] = both[0:OWN_ROWS, :]
        for n in range(NPAIR):
            out_ref[n, r : r + 1, :] = both[OWN_ROWS + n : OWN_ROWS + n + 1, :]
    for n in range(NPAIR):
        out_ref[n, 3:4, :] = jnp.zeros((1, 128), jnp.float32)


def returned_gradient(back_ref, cols_ref):
    high_iota = lax.broadcasted_iota(jnp.int32, (OWN_ROWS, 128), 0)
    low_iota = lax.broadcasted_iota(jnp.int32, (128, 128), 0)
    left_parts = []
    right_parts = []
    for n in range(NPAIR):
        cols = cols_ref[n : n + 1, :]
        chosen = high_iota == (cols >> 7)
        values = jnp.where(cols >= 0, back_ref[n], 0.0)
        lows = values - values.astype(jnp.bfloat16).astype(jnp.float32)
        stack = [jnp.where(chosen, values[r : r + 1, :], 0.0) for r in range(3)]
        stack += [jnp.where(chosen, lows[r : r + 1, :], 0.0) for r in range(3)]
        left_parts.append(jnp.concatenate(stack, axis=0).astype(jnp.bfloat16))
        right_parts.append(jnp.where(low_iota == (cols & 127), 1.0, 0.0).astype(jnp.bfloat16))
    out = nt_dot(jnp.concatenate(left_parts, axis=1), jnp.concatenate(right_parts, axis=1))
    return out[0:48, :] + out[48:96, :]


def moved(pos_ref, mask_ref, own_ref, back_ref, cols_ref):
    grad = own_ref[...] + returned_gradient(back_ref, cols_ref)
    free = jnp.where(mask_ref[...] == 0, STEP, 0.0)
    return pos_ref[...] - jnp.concatenate([free, free, free], axis=0) * grad


def load_positions(raw_ref, pos_ref):
    for r in range(3):
        for h in range(OWN_ROWS):
            pos_ref[r * OWN_ROWS + h : r * OWN_ROWS + h + 1, :] = raw_ref[r : r + 1, h * 128 : (h + 1) * 128]


def store_positions(value, raw_ref):
    for r in range(3):
        for h in range(OWN_ROWS):
            raw_ref[r : r + 1, h * 128 : (h + 1) * 128] = value[r * OWN_ROWS + h : r * OWN_ROWS + h + 1, :]


def start_kernel(raw_ref, list_ref, count_ref, nodes_ref, pos_ref, cols_ref, packed_ref, pay_ref):
    load_positions(raw_ref, pos_ref)
    send_columns(list_ref, count_ref, cols_ref)
    prepare_blocks(nodes_ref, packed_ref)
    gather_payload(pos_ref, cols_ref, pay_ref)


def gradient_kernel(pos_ref, ghost_ref, packed_ref, corners_ref, own_ref, out_ref, spread_ref, acc_ref):
    spread_ref[192:320, :] = jnp.zeros((128, 128), jnp.float32)
    local_gradient(pos_ref, ghost_ref, packed_ref, corners_ref, spread_ref, acc_ref)
    put_gradient(acc_ref, own_ref, out_ref)


def step_kernel(pos_ref, mask_ref, own_ref, back_ref, cols_ref, next_ref, pay_ref):
    next_ref[...] = moved(pos_ref, mask_ref, own_ref, back_ref, cols_ref)
    gather_payload(next_ref, cols_ref, pay_ref)


def last_kernel(pos_ref, mask_ref, own_ref, back_ref, cols_ref, raw_ref):
    store_positions(moved(pos_ref, mask_ref, own_ref, back_ref, cols_ref), raw_ref)


def partners(sign):
    dom = lax.axis_index("dom")
    sub = lax.axis_index("sub")
    doms = lax.axis_size("dom")
    found = []
    for k in range(SLOTS):
        for turn in range(SUBS):
            if k == REACH and turn == 0:
                continue
            there = lax.rem(dom + sign * (k - REACH) + doms, doms)
            found.append((k, turn, there, lax.rem(sub + turn, SUBS)))
    return found


def exchange_kernel(sign, src_ref, dst_ref, send_sem, recv_sem):
    sub = lax.axis_index("sub")
    found = partners(sign)
    barrier = pltpu.get_barrier_semaphore()
    for k, turn, there, t in found:
        pl.semaphore_signal(barrier, inc=1, device_id=(there, t), device_id_type=MESH)
    pl.semaphore_wait(barrier, len(found))
    copies = []
    for k, turn, there, t in found:
        copies.append(
            pltpu.make_async_remote_copy(
                src_ref=src_ref.at[k * SUBS + t],
                dst_ref=dst_ref.at[k * SUBS + sub],
                send_sem=send_sem.at[k * SUBS + turn],
                recv_sem=recv_sem.at[k * SUBS + turn],
                device_id=(there, t),
                device_id_type=MESH,
            )
        )
    for copy in copies:
        copy.start()
    dst_ref[REACH * SUBS + sub] = src_ref[REACH * SUBS + sub]
    for copy in copies:
        copy.wait()


VMEM = pl.BlockSpec(memory_space=pltpu.VMEM)
SMEM = pl.BlockSpec(memory_space=pltpu.SMEM)


def shape(*dims, dtype=jnp.float32):
    return jax.ShapeDtypeStruct(dims, dtype)


def exchange(value, sign):
    return pl.pallas_call(
        functools.partial(exchange_kernel, sign),
        out_shape=shape(NPAIR, 4, 128),
        in_specs=[VMEM],
        out_specs=VMEM,
        scratch_shapes=[pltpu.SemaphoreType.DMA((NPAIR,)), pltpu.SemaphoreType.DMA((NPAIR,))],
        compiler_params=pltpu.CompilerParams(collective_id=0 if sign > 0 else 1, has_side_effects=True),
        name="forward" if sign > 0 else "back",
    )(value)


def gradient(pos, ghosts, packed, corners):
    return pl.pallas_call(
        gradient_kernel,
        out_shape=(shape(48, 128), shape(NPAIR, 4, 128)),
        in_specs=[VMEM] * 4,
        out_specs=(VMEM, VMEM),
        scratch_shapes=[pltpu.VMEM((320, 128), jnp.float32), pltpu.VMEM((6 * HPAD, 128), jnp.float32)],
        name="gradient",
    )(pos, ghosts, packed, corners)


def per_device(positions, fixed_mask, send_count, send_list, block_nodes, tet_corners):
    corners = tet_corners.reshape(4, 128, 128).transpose(1, 0, 2).reshape(512, 128)
    mask = fixed_mask.reshape(OWN_ROWS, 128)
    pos, cols, packed, pay = pl.pallas_call(
        start_kernel,
        out_shape=(
            shape(48, 128),
            shape(NPAIR, 128, dtype=jnp.int32),
            shape(64, 128, dtype=jnp.int32),
            shape(NPAIR, 4, 128),
        ),
        in_specs=[VMEM, VMEM, SMEM, VMEM],
        out_specs=(VMEM,) * 4,
        name="start",
    )(positions, send_list, send_count, block_nodes)
    for step in range(ITERS):
        ghosts = exchange(pay, 1)
        own, out = gradient(pos, ghosts, packed, corners)
        back = exchange(out, -1)
        if step < ITERS - 1:
            pos, pay = pl.pallas_call(
                step_kernel,
                out_shape=(shape(48, 128), shape(NPAIR, 4, 128)),
                in_specs=[VMEM] * 5,
                out_specs=(VMEM,) * 2,
                name="step",
            )(pos, mask, own, back, cols)
    return pl.pallas_call(
        last_kernel,
        out_shape=shape(3, 2048),
        in_specs=[VMEM] * 5,
        out_specs=VMEM,
        name="last",
    )(pos, mask, own, back, cols)


def solution(mesh):
    return jax.shard_map(
        per_device,
        mesh=mesh,
        in_specs=(
            P(None, ("dom", "sub")),
            P(("dom", "sub")),
            P("dom", "sub", None, None),
            P("dom", "sub", None, None, None),
            P(None, ("dom", "sub")),
            P(None, ("dom", "sub")),
        ),
        out_specs=P(None, ("dom", "sub")),
        check_vma=False,
    )
```

time: 619 us -> 83.4 us (0.13)
  other arithmetic: 232 us -> 0 us
  local copies, waits for them, and re-layouts: 201 us -> 1.36 us
  Pallas kernels: 0 us -> 81.3 us
  starting transfers between devices: 81.3 us -> 0 us
  matrix products: 67.2 us -> 0 us
  waiting for transfers between devices: 24.2 us -> 0 us
  blocking collectives: 6.7 us -> 0 us
    scatter-add x4 -> x0, other arithmetic: 119 us -> none  [the longest x2 89.8 us: tet_energy(): block_coords = local_nodes[:, block_nodes.T]]
    pallas_call x0 -> x9, Pallas kernels: none -> 81.3 us  [the longest x4 56.4 us: exchange(): pl.pallas_call(functools.partial(exchange_kernel, sign), out_shape=shape(...]
    dynamic_update_slice x80 -> x0, local copies, waits for them, and re-layouts: 74.2 us -> none  [tet_energy(): return jnp.sum(lax.map(group_energy, (block_coords, corner_rows)))]
    gather x8 -> x0, local copies, waits for them, and re-layouts: 70.8 us -> none  [the longest x4 61.8 us: tet_energy(): block_coords = local_nodes[:, block_nodes.T]]
    ppermute x16 -> x0, starting transfers between devices: 70.7 us -> none  [from_behind(): return lax.ppermute(value, axis, pairs)]
    dot_general x32 -> x0, matrix products: 67.2 us -> none  [group_energy(): jnp.einsum('rgm,ngim->rngi', coords, incidence, precision=lax.Precision.H...]
    convert_element_type x16 -> x0, other arithmetic: 48.5 us -> none  [group_energy(): (rows[:, :, :, None] == column_ids[None, None, None, :]).astype(jnp.float32)]
    dynamic_update_slice x64 -> x0, other arithmetic: 30.8 us -> none  [tet_energy(): return jnp.sum(lax.map(group_energy, (block_coords, corner_rows)))]
  transfers between devices with their start and end apart: 19 -> 0, of which waited for: 8 -> 0; matrix products, arithmetic and copies ran while one was open for 0% -> 0% of each run, Pallas kernels for 0% -> 0%
where the time goes in v1:
time: 83.4 us; the launch traced here: 82.7 us
  Pallas kernels  81.3 us (97%)
  local copies, waits for them, and re-layouts  1.36 us (2%)
    pallas_call x4, Pallas kernels, exchange(): pl.pallas_call(functools.partial(exchange_kernel, sign), out_shape=shape(...  56.4 us
    pallas_call x2, Pallas kernels, gradient(): pl.pallas_call(gradient_kernel, out_shape=(shape(48, 128), shape(NPAIR, 4...  19 us
    pallas_call x1, Pallas kernels, per_device(): pl.pallas_call(step_kernel, out_shape=(shape(48, 128), shape(NPAIR, 4, 12...  2.2 us
    pallas_call x1, Pallas kernels, per_device(): pl.pallas_call(start_kernel, out_shape=(shape(48, 128), shape(NPAIR, 128,...  1.98 us
    pallas_call x1, Pallas kernels, per_device(): pl.pallas_call(last_kernel, out_shape=shape(3, 2048), in_specs=[VMEM] * 5...  1.78 us

profile of v1, /device:TPU:1, one launch (start us, length us, event | category | flops | bytes accessed | tf_op | source)
XLA Modules:
  0.0 82.7 jit_solution(13256003981207997633)
XLA Ops:
  0.0 0.0 copy-start
  0.0 0.7 copy-done
  0.7 0.7 copy.7.count_ref
  1.4 2.0 %start.1 = (f32[48,128]{1,0:T(8,128)}, s32[20,128]{1,0:T(8,128)}, s32[64,128]{1,0:T(8,128)}, f32[20,4,128]{2,1,0:T(4,128)}) custom-call(f32[3,2048]{1,0:T(4,128)} %raw_ref.1, s32[1,1,5,4,128]{4,3,2,1,0:T(4,128)} %list_ref.1, s32[1,1,5,4]{3,2,1,0:T(8,128)} %copy.7.count_ref, s32[64,128]{1,0:T(8,128)} %nodes_ref.1), custom_call_target="tpu_custom_call" | custom-call | tf_op jit(solution)/shard_map/start/pallas_call | solution.py:300
  3.3 20.8 %forward.2.ghost_ref = f32[20,4,128]{2,1,0:T(4,128)} custom-call(f32[20,4,128]{2,1,0:T(4,128)} %get-tuple-element.16.src_ref), custom_call_target="tpu_custom_call" | custom-call | tf_op jit(solution)/shard_map/forward/pallas_call | solution.py:275
  24.1 9.5 %gradient.2 = (f32[48,128]{1,0:T(8,128)}, f32[20,4,128]{2,1,0:T(4,128)}) custom-call(f32[48,128]{1,0:T(8,128)} %get-tuple-element.15.pos_ref, f32[20,4,128]{2,1,0:T(4,128)} %forward.2.ghost_ref, s32[64,128]{1,0:T(8,128)} %get-tuple-element.17.packed_ref, s32[512,128]{1,0:T(8,128)} %bitcast.6), custom_call_target="tpu_custom_call" | custom-call | tf_op jit(solution)/shard_map/gradient/pallas_call | solution.py:287
  33.6 11.9 %back.2.back_ref = f32[20,4,128]{2,1,0:T(4,128)} custom-call(f32[20,4,128]{2,1,0:T(4,128)} %get-tuple-element.19.src_ref), custom_call_target="tpu_custom_call" | custom-call | tf_op jit(solution)/shard_map/back/pallas_call | solution.py:275
  45.6 2.2 %step.1 = (f32[48,128]{1,0:T(8,128)}, f32[20,4,128]{2,1,0:T(4,128)}) custom-call(f32[48,128]{1,0:T(8,128)} %get-tuple-element.15.pos_ref, s32[16,128]{1,0:T(8,128)} %bitcast.8, f32[48,128]{1,0:T(8,128)} %get-tuple-element.18.own_ref, f32[20,4,128]{2,1,0:T(4,128)} %back.2.back_ref, s32[20,128]{1,0:T(8,128)} %get-tuple-element.20.cols_ref), custom_call_target="tpu_custom_call" | custom-call | tf_op jit(solution)/shard_map/step/pallas_call | solution.py:317
  47.8 11.9 %forward.3.ghost_ref = f32[20,4,128]{2,1,0:T(4,128)} custom-call(f32[20,4,128]{2,1,0:T(4,128)} %get-tuple-element.22.src_ref), custom_call_target="tpu_custom_call" | custom-call | tf_op jit(solution)/shard_map/forward/pallas_call | solution.py:275
  59.7 9.5 %gradient.3 = (f32[48,128]{1,0:T(8,128)}, f32[20,4,128]{2,1,0:T(4,128)}) custom-call(f32[48,128]{1,0:T(8,128)} %get-tuple-element.21.pos_ref, f32[20,4,128]{2,1,0:T(4,128)} %forward.3.ghost_ref, s32[64,128]{1,0:T(8,128)} %get-tuple-element.17.packed_ref, s32[512,128]{1,0:T(8,128)} %bitcast.7), custom_call_target="tpu_custom_call" | custom-call | tf_op jit(solution)/shard_map/gradient/pallas_call | solution.py:287
  69.2 11.8 %back.3.back_ref = f32[20,4,128]{2,1,0:T(4,128)} custom-call(f32[20,4,128]{2,1,0:T(4,128)} %get-tuple-element.24.src_ref), custom_call_target="tpu_custom_call" | custom-call | tf_op jit(solution)/shard_map/back/pallas_call | solution.py:275
  81.0 1.8 %last.1 = f32[3,2048]{1,0:T(4,128)} custom-call(f32[48,128]{1,0:T(8,128)} %get-tuple-element.21.pos_ref, s32[16,128]{1,0:T(8,128)} %bitcast.9, f32[48,128]{1,0:T(8,128)} %get-tuple-element.23.own_ref, f32[20,4,128]{2,1,0:T(4,128)} %back.3.back_ref, s32[20,128]{1,0:T(8,128)} %get-tuple-element.20.cols_ref), custom_call_target="tpu_custom_call" | custom-call | tf_op jit(solution)/shard_map/last/pallas_call | solution.py:324
Async XLA Ops:
  0.0 0.7 copy-start

commit v2 on v1

--- a/solution.py
+++ b/solution.py
@@ -1,4 +1,3 @@
-import functools
 import math
 
 import jax
@@ -201,28 +200,6 @@
             raw_ref[r : r + 1, h * 128 : (h + 1) * 128] = value[r * OWN_ROWS + h : r * OWN_ROWS + h + 1, :]
 
 
-def start_kernel(raw_ref, list_ref, count_ref, nodes_ref, pos_ref, cols_ref, packed_ref, pay_ref):
-    load_positions(raw_ref, pos_ref)
-    send_columns(list_ref, count_ref, cols_ref)
-    prepare_blocks(nodes_ref, packed_ref)
-    gather_payload(pos_ref, cols_ref, pay_ref)
-
-
-def gradient_kernel(pos_ref, ghost_ref, packed_ref, corners_ref, own_ref, out_ref, spread_ref, acc_ref):
-    spread_ref[192:320, :] = jnp.zeros((128, 128), jnp.float32)
-    local_gradient(pos_ref, ghost_ref, packed_ref, corners_ref, spread_ref, acc_ref)
-    put_gradient(acc_ref, own_ref, out_ref)
-
-
-def step_kernel(pos_ref, mask_ref, own_ref, back_ref, cols_ref, next_ref, pay_ref):
-    next_ref[...] = moved(pos_ref, mask_ref, own_ref, back_ref, cols_ref)
-    gather_payload(next_ref, cols_ref, pay_ref)
-
-
-def last_kernel(pos_ref, mask_ref, own_ref, back_ref, cols_ref, raw_ref):
-    store_positions(moved(pos_ref, mask_ref, own_ref, back_ref, cols_ref), raw_ref)
-
-
 def partners(sign):
     dom = lax.axis_index("dom")
     sub = lax.axis_index("sub")
@@ -237,13 +214,8 @@
     return found
 
 
-def exchange_kernel(sign, src_ref, dst_ref, send_sem, recv_sem):
+def exchange(sign, found, src_ref, dst_ref, send_sem, recv_sem):
     sub = lax.axis_index("sub")
-    found = partners(sign)
-    barrier = pltpu.get_barrier_semaphore()
-    for k, turn, there, t in found:
-        pl.semaphore_signal(barrier, inc=1, device_id=(there, t), device_id_type=MESH)
-    pl.semaphore_wait(barrier, len(found))
     copies = []
     for k, turn, there, t in found:
         copies.append(
@@ -263,71 +235,81 @@
         copy.wait()
 
 
+def smooth_kernel(
+    raw_ref,
+    mask_ref,
+    list_ref,
+    count_ref,
+    nodes_ref,
+    corners_ref,
+    done_ref,
+    pos_ref,
+    cols_ref,
+    packed_ref,
+    pay_ref,
+    ghost_ref,
+    out_ref,
+    back_ref,
+    own_ref,
+    spread_ref,
+    acc_ref,
+    send_sem,
+    recv_sem,
+):
+    ahead = partners(1)
+    behind = partners(-1)
+    barrier = pltpu.get_barrier_semaphore()
+    for _, _, there, t in ahead:
+        pl.semaphore_signal(barrier, inc=1, device_id=(there, t), device_id_type=MESH)
+    load_positions(raw_ref, pos_ref)
+    send_columns(list_ref, count_ref, cols_ref)
+    prepare_blocks(nodes_ref, packed_ref)
+    spread_ref[192:320, :] = jnp.zeros((128, 128), jnp.float32)
+    gather_payload(pos_ref, cols_ref, pay_ref.at[0])
+    pl.semaphore_wait(barrier, len(ahead))
+    for step in range(ITERS):
+        exchange(1, ahead, pay_ref.at[step], ghost_ref.at[step], send_sem.at[2 * step], recv_sem.at[2 * step])
+        local_gradient(pos_ref, ghost_ref.at[step], packed_ref, corners_ref, spread_ref, acc_ref)
+        put_gradient(acc_ref, own_ref, out_ref.at[step])
+        exchange(-1, behind, out_ref.at[step], back_ref.at[step], send_sem.at[2 * step + 1], recv_sem.at[2 * step + 1])
+        value = moved(pos_ref, mask_ref, own_ref, back_ref.at[step], cols_ref)
+        if step < ITERS - 1:
+            pos_ref[...] = value
+            gather_payload(pos_ref, cols_ref, pay_ref.at[step + 1])
+        else:
+            store_positions(value, done_ref)
+
+
 VMEM = pl.BlockSpec(memory_space=pltpu.VMEM)
 SMEM = pl.BlockSpec(memory_space=pltpu.SMEM)
-
-
-def shape(*dims, dtype=jnp.float32):
-    return jax.ShapeDtypeStruct(dims, dtype)
-
-
-def exchange(value, sign):
-    return pl.pallas_call(
-        functools.partial(exchange_kernel, sign),
-        out_shape=shape(NPAIR, 4, 128),
-        in_specs=[VMEM],
-        out_specs=VMEM,
-        scratch_shapes=[pltpu.SemaphoreType.DMA((NPAIR,)), pltpu.SemaphoreType.DMA((NPAIR,))],
-        compiler_params=pltpu.CompilerParams(collective_id=0 if sign > 0 else 1, has_side_effects=True),
-        name="forward" if sign > 0 else "back",
-    )(value)
-
-
-def gradient(pos, ghosts, packed, corners):
-    return pl.pallas_call(
-        gradient_kernel,
-        out_shape=(shape(48, 128), shape(NPAIR, 4, 128)),
-        in_specs=[VMEM] * 4,
-        out_specs=(VMEM, VMEM),
-        scratch_shapes=[pltpu.VMEM((320, 128), jnp.float32), pltpu.VMEM((6 * HPAD, 128), jnp.float32)],
-        name="gradient",
-    )(pos, ghosts, packed, corners)
 
 
 def per_device(positions, fixed_mask, send_count, send_list, block_nodes, tet_corners):
     corners = tet_corners.reshape(4, 128, 128).transpose(1, 0, 2).reshape(512, 128)
     mask = fixed_mask.reshape(OWN_ROWS, 128)
-    pos, cols, packed, pay = pl.pallas_call(
-        start_kernel,
-        out_shape=(
-            shape(48, 128),
-            shape(NPAIR, 128, dtype=jnp.int32),
-            shape(64, 128, dtype=jnp.int32),
-            shape(NPAIR, 4, 128),
-        ),
-        in_specs=[VMEM, VMEM, SMEM, VMEM],
-        out_specs=(VMEM,) * 4,
-        name="start",
-    )(positions, send_list, send_count, block_nodes)
-    for step in range(ITERS):
-        ghosts = exchange(pay, 1)
-        own, out = gradient(pos, ghosts, packed, corners)
-        back = exchange(out, -1)
-        if step < ITERS - 1:
-            pos, pay = pl.pallas_call(
-                step_kernel,
-                out_shape=(shape(48, 128), shape(NPAIR, 4, 128)),
-                in_specs=[VMEM] * 5,
-                out_specs=(VMEM,) * 2,
-                name="step",
-            )(pos, mask, own, back, cols)
+    slots = pltpu.VMEM((ITERS, NPAIR, 4, 128), jnp.float32)
     return pl.pallas_call(
-        last_kernel,
-        out_shape=shape(3, 2048),
-        in_specs=[VMEM] * 5,
+        smooth_kernel,
+        out_shape=jax.ShapeDtypeStruct((3, 2048), jnp.float32),
+        in_specs=[VMEM, VMEM, VMEM, SMEM, VMEM, VMEM],
         out_specs=VMEM,
-        name="last",
-    )(pos, mask, own, back, cols)
+        scratch_shapes=[
+            pltpu.VMEM((48, 128), jnp.float32),
+            pltpu.VMEM((NPAIR, 128), jnp.int32),
+            pltpu.VMEM((64, 128), jnp.int32),
+            slots,
+            slots,
+            slots,
+            slots,
+            pltpu.VMEM((48, 128), jnp.float32),
+            pltpu.VMEM((320, 128), jnp.float32),
+            pltpu.VMEM((6 * HPAD, 128), jnp.float32),
+            pltpu.SemaphoreType.DMA((2 * ITERS, NPAIR)),
+            pltpu.SemaphoreType.DMA((2 * ITERS, NPAIR)),
+        ],
+        compiler_params=pltpu.CompilerParams(collective_id=0, has_side_effects=True),
+        name="smooth",
+    )(positions, mask, send_list, send_count, block_nodes, corners)
 
 
 def solution(mesh):

time: 83.4 us -> 60.5 us (0.73)
  Pallas kernels: 81.3 us -> 57.6 us
  local copies, waits for them, and re-layouts: 1.36 us -> 2.74 us
    pallas_call x9 -> x1, Pallas kernels: 81.3 us -> 57.6 us  [per_device(): pl.pallas_call(smooth_kernel, out_shape=jax.ShapeDtypeStruct((3, 2048), j...]
    unnamed x3 -> x4, local copies, waits for them, and re-layouts: 1.36 us -> 2.74 us
where the time goes in v2:
time: 60.5 us; the launch traced here: 60.3 us
  Pallas kernels  57.6 us (95%)
  local copies, waits for them, and re-layouts  2.74 us (5%)
    pallas_call x1, Pallas kernels, per_device(): pl.pallas_call(smooth_kernel, out_shape=jax.ShapeDtypeStruct((3, 2048), j...  57.6 us
    unnamed x4, local copies, waits for them, and re-layouts  2.74 us

profile of v2, /device:TPU:1, one launch (start us, length us, event | category | flops | bytes accessed | tf_op | source)
XLA Modules:
  0.0 60.3 jit_solution(11166629515538851985)
XLA Ops:
  0.0 0.0 copy-start
  0.0 0.7 %copy-done = s32[1,1,5,4]{2,3,1,0:T(4,128)S(1)} copy-done((s32[1,1,5,4]{2,3,1,0:T(4,128)S(1)}, s32[1,1,5,4]{2,3,1,0:T(4,128)}, u32[]{:S(2)}) %copy-start) | copy-done | bytes 104
  0.7 0.7 %copy.8.count_ref = s32[1,1,5,4]{3,2,1,0:T(8,128)} copy(s32[1,1,5,4]{2,3,1,0:T(4,128)S(1)} %copy-done) | data formatting | bytes 160 | tf_op args[2]
  1.4 57.6 %smooth.1 = f32[3,2048]{1,0:T(4,128)} custom-call(f32[3,2048]{1,0:T(4,128)} %raw_ref.1, s32[16,128]{1,0:T(8,128)} %bitcast.7, s32[1,1,5,4,128]{4,3,2,1,0:T(4,128)} %list_ref.1, s32[1,1,5,4]{3,2,1,0:T(8,128)} %copy.8.count_ref, s32[64,128]{1,0:T(8,128)} %nodes_ref.1, s32[512,128]{1,0:T(8,128)} %bitcast.6), custom_call_target="tpu_custom_call" | custom-call | tf_op jit(solution)/shard_map/smooth/pallas_call | solution.py:291
  58.9 1.4 %copy.10 = f32[3,2048]{1,0:T(4,128)} copy(f32[3,2048]{1,0:T(4,128)} %smooth.1) | data formatting | bytes 49152
Async XLA Ops:
  0.0 0.7 %copy-start = (s32[1,1,5,4]{2,3,1,0:T(4,128)S(1)}, s32[1,1,5,4]{2,3,1,0:T(4,128)}, u32[]{:S(2)}) copy-start(s32[1,1,5,4]{2,3,1,0:T(4,128)} %param.8) | copy-start | bytes 244

commit v3 on v2

v3 whole, which is shorter than its diff:
```python
import functools
import math

import jax
import jax.numpy as jnp
from jax import lax
from jax.experimental import pallas as pl
from jax.experimental.pallas import tpu as pltpu
from jax.sharding import PartitionSpec as P

ITERS = 2
STEP = 0.01
DELTA = 2.0
REACH = 2
SLOTS = 5
SUBS = 4
NPAIR = SLOTS * SUBS
OWN_ROWS = 16
ROWS = OWN_ROWS + NPAIR
GPAD = 24
GROUPS = 4
MESH = pl.DeviceIdType.MESH


def nt_dot(a, b):
    return lax.dot_general(a, b, (((1,), (1,)), ((), ())), preferred_element_type=jnp.float32)


def low_piece(x):
    return x - x.astype(jnp.bfloat16).astype(jnp.float32)


def lane_take(row, lanes):
    src = jnp.broadcast_to(row, lanes.shape)
    return jnp.take_along_axis(src, lanes, axis=1, mode="promise_in_bounds")


def send_columns(list_ref, count_ref, cols_ref):
    lane = lax.broadcasted_iota(jnp.int32, (1, 128), 1)
    for k in range(SLOTS):
        for t in range(SUBS):
            count = jnp.broadcast_to(count_ref[0, 0, t : t + 1, k : k + 1], (1, 128))
            row = list_ref[0, 0, k, t : t + 1, :]
            cols_ref[k * SUBS + t : k * SUBS + t + 1, :] = jnp.where(lane < count, row, -1)


def gather_payload(pos_ref, cols_ref, pay_ref):
    cols = jnp.concatenate([cols_ref[...], jnp.full((24 - NPAIR, 128), -1, jnp.int32)], axis=0)
    high = cols >> 7
    low = cols & 127
    for r in range(3):
        acc = jnp.zeros((24, 128), jnp.float32)
        for h in range(OWN_ROWS):
            picked = lane_take(pos_ref[r * OWN_ROWS + h : r * OWN_ROWS + h + 1, :], low)
            acc = jnp.where(high == h, picked, acc)
        for n in range(NPAIR):
            pay_ref[n, r : r + 1, :] = acc[n : n + 1, :]


def tet_gradient(corner):
    edge = [[corner[m + 1][r] - corner[0][r] for r in range(3)] for m in range(3)]
    total = [edge[0][r] + edge[1][r] + edge[2][r] for r in range(3)]
    squares = None
    for m in range(3):
        for r in range(3):
            term = edge[m][r] * edge[m][r]
            squares = term if squares is None else squares + term
    spread = total[0] * total[0] + total[1] * total[1] + total[2] * total[2]
    norm_sq = 2.0 * squares - 0.5 * spread

    def cross(a, b):
        return [
            a[1] * b[2] - a[2] * b[1],
            a[2] * b[0] - a[0] * b[2],
            a[0] * b[1] - a[1] * b[0],
        ]

    cof = [cross(edge[1], edge[2]), cross(edge[2], edge[0]), cross(edge[0], edge[1])]
    root2 = math.sqrt(2.0)
    det = root2 * (edge[0][0] * cof[0][0] + edge[0][1] * cof[0][1] + edge[0][2] * cof[0][2])
    root = jnp.sqrt(det * det + 4.0 * DELTA * DELTA)
    far = root + jnp.abs(det)
    height = jnp.where(det >= 0, 0.5 * far, (2.0 * DELTA * DELTA) / far)
    factor = (2.0 / 3.0) * jnp.exp((-2.0 / 3.0) * jnp.log(height))
    pull = (root2 / 3.0) * norm_sq / root
    grads = []
    for m in range(3):
        grads.append([factor * (2.0 * edge[m][r] - 0.5 * total[r] - pull * cof[m][r]) for r in range(3)])
    first = [-(grads[0][r] + grads[1][r] + grads[2][r]) for r in range(3)]
    return [first] + grads


def prepare_blocks(nodes_ref, packed_ref):
    turned = nodes_ref[...].T
    packed_ref[...] = jnp.concatenate([turned[0:64, :], turned[64:128, :]], axis=1)


def mark(chosen):
    return jnp.where(chosen, 1.0, 0.0).astype(jnp.bfloat16)


def build_marks(packed_ref, corners_ref, cols_ref, marks_ref, lanes_ref, slots_ref):
    node_iota = lax.broadcasted_iota(jnp.int32, (64, 128), 0)
    lane_iota = lax.broadcasted_iota(jnp.int32, (128, 128), 0)

    def corner_marks(g, carry):
        for i in range(4):
            block = g * 4 + i
            for c in range(4):
                ids = corners_ref[pl.ds(block * 4 + c, 1), :]
                marks_ref[block, :, c * 128 : (c + 1) * 128] = mark(node_iota == ids)
        return carry

    lax.fori_loop(0, 32, corner_marks, 0)

    def lane_marks(j, carry):
        low = packed_ref[pl.ds(pl.multiple_of(j * 8, 8), 8), :] & 127
        for i in range(8):
            lanes_ref[j, :, i * 128 : (i + 1) * 128] = mark(lane_iota == low[i : i + 1, :])
        return carry

    lax.fori_loop(0, 8, lane_marks, 0)
    for n in range(NPAIR):
        slots_ref[:, n * 128 : (n + 1) * 128] = mark(lane_iota == (cols_ref[n : n + 1, :] & 127))


def gather_own(pos_ref, packed_ref, part_ref):
    def body(g, carry):
        for i in range(2):
            rows = pl.ds(pl.multiple_of(g * 16 + i * 8, 8), 8)
            cols = packed_ref[rows, :]
            high = cols >> 7
            low = cols & 127
            for r in range(3):
                picked = jnp.zeros((8, 128), jnp.float32)
                for h in range(OWN_ROWS):
                    row = pos_ref[r * OWN_ROWS + h : r * OWN_ROWS + h + 1, :]
                    picked = jnp.where(high == h, lane_take(row, low), picked)
                part_ref[r, rows, :] = picked
        return carry

    lax.fori_loop(0, GROUPS, body, 0)


def tet_spread(j, ghost_ref, packed_ref, part_ref, corners_ref, spread_ref):
    base = pl.multiple_of(j * 8, 8)
    cols = packed_ref[pl.ds(base, 8), :]
    high = cols >> 7
    low = cols & 127
    source = []
    for r in range(3):
        picked = part_ref[r, pl.ds(base, 8), :]
        for n in range(NPAIR):
            picked = jnp.where(high == OWN_ROWS + n, lane_take(ghost_ref[n, r : r + 1, :], low), picked)
        source.append(picked)
    for half in range(2):
        block = half * 64 + base
        corner = []
        for c in range(4):
            lanes = corners_ref[pl.ds(block * 4 + c, 8, stride=4), :] + 64 * half
            corner.append([jnp.take_along_axis(source[r], lanes, axis=1, mode="promise_in_bounds") for r in range(3)])
        grads = tet_gradient(corner)
        for c in range(4):
            for r in range(3):
                start = (c * 6 + r) * 16 + half * 8
                spread_ref[start : start + 8, :] = grads[c][r]
                spread_ref[start + 48 : start + 56, :] = low_piece(grads[c][r])


def block_sums(j, spread_ref, marks_ref, pairs_ref):
    found = []
    for i in range(8):
        sums = []
        for half in range(2):
            rows = [
                spread_ref[pl.ds(c * 96 + half * 8 + i, 8, stride=16), :].astype(jnp.bfloat16) for c in range(4)
            ]
            sums.append(nt_dot(jnp.concatenate(rows, axis=1), marks_ref[half * 64 + j * 8 + i]))
        both = jnp.concatenate(sums, axis=1)
        pair = both[0:3, :] + both[3:6, :]
        pairs_ref[j * 8 + i, 0:3, :] = pair
        found.append(pair)
    return found


def row_group(j, pairs, packed_ref, lanes_ref, first, count):
    row_iota = lax.broadcasted_iota(jnp.int32, (count, 128), 0) + first
    high = packed_ref[pl.ds(pl.multiple_of(j * 8, 8), 8), :] >> 7
    left = []
    for i in range(8):
        pair = pairs[i]
        rest = low_piece(pair)
        chosen = row_iota == high[i : i + 1, :]
        stack = [jnp.where(chosen, pair[r : r + 1, :], 0.0) for r in range(3)]
        stack += [jnp.where(chosen, rest[r : r + 1, :], 0.0) for r in range(3)]
        left.append(jnp.concatenate(stack, axis=0).astype(jnp.bfloat16))
    return nt_dot(jnp.concatenate(left, axis=1), lanes_ref[j])


def ghost_rows(ghost_ref, packed_ref, part_ref, corners_ref, spreads, marks_ref, lanes_ref, pairs_ref, acc_ref):
    even_ref, odd_ref = spreads
    tets = functools.partial(tet_spread, ghost_ref=ghost_ref, packed_ref=packed_ref, part_ref=part_ref)

    def body(g, carry):
        pairs = block_sums(2 * g, even_ref, marks_ref, pairs_ref)
        tets(2 * g + 1, corners_ref=corners_ref, spread_ref=odd_ref)
        first = row_group(2 * g, pairs, packed_ref, lanes_ref, OWN_ROWS, GPAD)
        pairs = block_sums(2 * g + 1, odd_ref, marks_ref, pairs_ref)
        tets(jnp.minimum(2 * g + 2, 7), corners_ref=corners_ref, spread_ref=even_ref)
        second = row_group(2 * g + 1, pairs, packed_ref, lanes_ref, OWN_ROWS, GPAD)
        acc_ref[...] += first + second
        return carry

    acc_ref[...] = jnp.zeros_like(acc_ref)
    tets(0, corners_ref=corners_ref, spread_ref=even_ref)
    lax.fori_loop(0, 4, body, 0)


def own_rows(packed_ref, pairs_ref, lanes_ref, acc_ref):
    def body(g, carry):
        parts = []
        for half in range(2):
            j = 2 * g + half
            pairs = [pairs_ref[j * 8 + i, 0:3, :] for i in range(8)]
            parts.append(row_group(j, pairs, packed_ref, lanes_ref, 0, OWN_ROWS))
        acc_ref[...] += parts[0] + parts[1]
        return carry

    acc_ref[...] = jnp.zeros_like(acc_ref)
    lax.fori_loop(0, 4, body, 0)


def put_ghost_gradient(acc_ref, out_ref):
    for r in range(3):
        both = acc_ref[r * GPAD : (r + 1) * GPAD, :] + acc_ref[(3 + r) * GPAD : (4 + r) * GPAD, :]
        for n in range(NPAIR):
            out_ref[n, r : r + 1, :] = both[n : n + 1, :]


def returned_gradient(back_ref, cols_ref, slots_ref):
    high_iota = lax.broadcasted_iota(jnp.int32, (OWN_ROWS, 128), 0)
    left_parts = []
    for n in range(NPAIR):
        cols = cols_ref[n : n + 1, :]
        chosen = high_iota == (cols >> 7)
        values = jnp.where(cols >= 0, back_ref[n, 0:3, :], 0.0)
        rest = low_piece(values)
        stack = [jnp.where(chosen, values[r : r + 1, :], 0.0) for r in range(3)]
        stack += [jnp.where(chosen, rest[r : r + 1, :], 0.0) for r in range(3)]
        left_parts.append(jnp.concatenate(stack, axis=0).astype(jnp.bfloat16))
    out = nt_dot(jnp.concatenate(left_parts, axis=1), slots_ref[...])
    return out[0:48, :] + out[48:96, :]


def load_positions(raw_ref, pos_ref):
    for r in range(3):
        for h in range(OWN_ROWS):
            pos_ref[r * OWN_ROWS + h : r * OWN_ROWS + h + 1, :] = raw_ref[r : r + 1, h * 128 : (h + 1) * 128]


def store_positions(value, raw_ref):
    for r in range(3):
        for h in range(OWN_ROWS):
            raw_ref[r : r + 1, h * 128 : (h + 1) * 128] = value[r * OWN_ROWS + h : r * OWN_ROWS + h + 1, :]


FAR_FIRST = (2, 1, 3, 0)


def partners(sign):
    dom = lax.axis_index("dom")
    sub = lax.axis_index("sub")
    doms = lax.axis_size("dom")
    found = []
    for turn in FAR_FIRST:
        for k in (0, 4, 1, 3, 2):
            if k == REACH and turn == 0:
                continue
            there = lax.rem(dom + sign * (k - REACH) + doms, doms)
            found.append((k, turn, there, lax.rem(sub + turn, SUBS)))
    return found


def exchange(found, src_ref, dst_ref, send_sem, recv_sem):
    sub = lax.axis_index("sub")
    copies = []
    for k, turn, there, t in found:
        copies.append(
            pltpu.make_async_remote_copy(
                src_ref=src_ref.at[k * SUBS + t],
                dst_ref=dst_ref.at[k * SUBS + sub],
                send_sem=send_sem.at[k * SUBS + turn],
                recv_sem=recv_sem.at[k * SUBS + turn],
                device_id=(there, t),
                device_id_type=MESH,
            )
        )
    for copy in copies:
        copy.start()
    dst_ref[REACH * SUBS + sub] = src_ref[REACH * SUBS + sub]
    return copies


def smooth_kernel(
    raw_hbm,
    mask_hbm,
    list_hbm,
    count_hbm,
    nodes_hbm,
    corners_hbm,
    done_ref,
    raw_ref,
    mask_ref,
    list_ref,
    count_ref,
    nodes_ref,
    corners_ref,
    pos_ref,
    cols_ref,
    packed_ref,
    pay_ref,
    ghost_ref,
    out_ref,
    back_ref,
    part_ref,
    even_ref,
    odd_ref,
    marks_ref,
    lanes_ref,
    slots_ref,
    pairs_ref,
    ghost_acc,
    own_acc,
    load_sem,
    send_sem,
    recv_sem,
):
    ahead = partners(1)
    behind = partners(-1)
    barrier = pltpu.get_barrier_semaphore()
    for _, _, there, t in ahead:
        pl.semaphore_signal(barrier, inc=1, device_id=(there, t), device_id_type=MESH)
    sources = (raw_hbm, list_hbm, count_hbm, nodes_hbm, mask_hbm, corners_hbm)
    targets = (raw_ref, list_ref, count_ref, nodes_ref, mask_ref, corners_ref)
    loads = [pltpu.make_async_copy(sources[i], targets[i], load_sem.at[i]) for i in range(6)]
    for load in loads:
        load.start()
    for step in range(ITERS):
        for n in range(NPAIR):
            pay_ref[step, n, 3:4, :] = jnp.zeros((1, 128), jnp.float32)
            out_ref[step, n, 3:4, :] = jnp.zeros((1, 128), jnp.float32)
    for spread_ref in (even_ref, odd_ref):
        spread_ref[24 * 16 : 26 * 16, :] = jnp.zeros((32, 128), jnp.float32)
    for load in loads[0:3]:
        load.wait()
    load_positions(raw_ref, pos_ref)
    send_columns(list_ref, count_ref, cols_ref)
    gather_payload(pos_ref, cols_ref, pay_ref.at[0])
    for load in loads[3:6]:
        load.wait()
    pl.semaphore_wait(barrier, len(ahead))
    started = []
    for step in range(ITERS):
        copies = exchange(ahead, pay_ref.at[step], ghost_ref.at[step], send_sem.at[2 * step], recv_sem.at[2 * step])
        started += copies
        if step == 0:
            prepare_blocks(nodes_ref, packed_ref)
            build_marks(packed_ref, corners_ref, cols_ref, marks_ref, lanes_ref, slots_ref)
        gather_own(pos_ref, packed_ref, part_ref)
        for copy in copies:
            copy.wait_recv()
        ghost_rows(
            ghost_ref.at[step],
            packed_ref,
            part_ref,
            corners_ref,
            (even_ref, odd_ref),
            marks_ref,
            lanes_ref,
            pairs_ref,
            ghost_acc,
        )
        put_ghost_gradient(ghost_acc, out_ref.at[step])
        copies = exchange(
            behind, out_ref.at[step], back_ref.at[step], send_sem.at[2 * step + 1], recv_sem.at[2 * step + 1]
        )
        started += copies
        own_rows(packed_ref, pairs_ref, lanes_ref, own_acc)
        own = own_acc[0:48, :] + own_acc[48:96, :]
        free = jnp.where(mask_ref[...] == 0, STEP, 0.0)
        for copy in copies:
            copy.wait_recv()
        grad = own + returned_gradient(back_ref.at[step], cols_ref, slots_ref)
        value = pos_ref[...] - jnp.concatenate([free, free, free], axis=0) * grad
        if step < ITERS - 1:
            pos_ref[...] = value
            gather_payload(pos_ref, cols_ref, pay_ref.at[step + 1])
        else:
            store_positions(value, done_ref)
    for copy in started:
        copy.wait_send()


ANY = pl.BlockSpec(memory_space=pl.ANY)
VMEM = pl.BlockSpec(memory_space=pltpu.VMEM)


def per_device(positions, fixed_mask, send_count, send_list, block_nodes, tet_corners):
    corners = tet_corners.reshape(4, 128, 128).transpose(1, 0, 2).reshape(512, 128)
    mask = fixed_mask.reshape(OWN_ROWS, 128)
    counts = send_count.transpose(0, 1, 3, 2)
    inputs = (positions, mask, send_list, counts, block_nodes, corners)
    slots = pltpu.VMEM((ITERS, NPAIR, 4, 128), jnp.float32)
    return pl.pallas_call(
        smooth_kernel,
        out_shape=jax.ShapeDtypeStruct((3, 2048), jnp.float32),
        in_specs=[ANY] * 6,
        out_specs=VMEM,
        scratch_shapes=[pltpu.VMEM(x.shape, x.dtype) for x in inputs]
        + [
            pltpu.VMEM((48, 128), jnp.float32),
            pltpu.VMEM((NPAIR, 128), jnp.int32),
            pltpu.VMEM((64, 128), jnp.int32),
            slots,
            slots,
            slots,
            slots,
            pltpu.VMEM((3, 64, 128), jnp.float32),
            pltpu.VMEM((26 * 16, 128), jnp.float32),
            pltpu.VMEM((26 * 16, 128), jnp.float32),
            pltpu.VMEM((128, 64, 512), jnp.bfloat16),
            pltpu.VMEM((8, 128, 1024), jnp.bfloat16),
            pltpu.VMEM((128, NPAIR * 128), jnp.bfloat16),
            pltpu.VMEM((64, 8, 128), jnp.float32),
            pltpu.VMEM((6 * GPAD, 128), jnp.float32),
            pltpu.VMEM((6 * OWN_ROWS, 128), jnp.float32),
            pltpu.SemaphoreType.DMA((6,)),
            pltpu.SemaphoreType.DMA((2 * ITERS, NPAIR)),
            pltpu.SemaphoreType.DMA((2 * ITERS, NPAIR)),
        ],
        compiler_params=pltpu.CompilerParams(collective_id=0, has_side_effects=True),
        name="smooth",
    )(*inputs)


def solution(mesh):
    return jax.shard_map(
        per_device,
        mesh=mesh,
        in_specs=(
            P(None, ("dom", "sub")),
            P(("dom", "sub")),
            P("dom", "sub", None, None),
            P("dom", "sub", None, None, None),
            P(None, ("dom", "sub")),
            P(None, ("dom", "sub")),
        ),
        out_specs=P(None, ("dom", "sub")),
        check_vma=False,
    )
```

time: 60.5 us -> 51.1 us (0.84)
  Pallas kernels: 57.6 us -> 49.5 us
  local copies, waits for them, and re-layouts: 2.74 us -> 1.38 us
    pallas_call x1, Pallas kernels: 57.6 us -> 49.5 us  [per_device(): pl.pallas_call(smooth_kernel, out_shape=jax.ShapeDtypeStruct((3, 2048), j...]
    unnamed x4 -> x1, local copies, waits for them, and re-layouts: 2.74 us -> 1.38 us
where the time goes in v3:
time: 51.1 us; the launch traced here: 50.9 us
  Pallas kernels  49.5 us (97%)
  local copies, waits for them, and re-layouts  1.38 us (3%)
    pallas_call x1, Pallas kernels, per_device(): pl.pallas_call(smooth_kernel, out_shape=jax.ShapeDtypeStruct((3, 2048), j...  49.5 us
    unnamed x1, local copies, waits for them, and re-layouts  1.38 us

profile of v3, /device:TPU:1, one launch (start us, length us, event | category | flops | bytes accessed | tf_op | source)
XLA Modules:
  0.0 50.9 jit_solution(3746738611932168539)
XLA Ops:
  0.0 49.5 %smooth.1 = f32[3,2048]{1,0:T(4,128)} custom-call(f32[3,2048]{1,0:T(4,128)} %raw_hbm.1, s32[16,128]{1,0:T(8,128)} %bitcast.8, s32[1,1,5,4,128]{4,3,2,1,0:T(4,128)} %list_hbm.1, s32[1,1,4,5]{3,2,1,0:T(4,128)} %bitcast.9, s32[64,128]{1,0:T(8,128)} %nodes_hbm.1, s32[512,128]{1,0:T(8,128)} %bitcast.7), custom_call_target="tpu_custom_call" | custom-call | tf_op jit(solution)/shard_map/smooth/pallas_call | solution.py:414
  49.5 1.4 %copy.9 = f32[3,2048]{1,0:T(4,128)} copy(f32[3,2048]{1,0:T(4,128)} %smooth.1) | data formatting | bytes 49152

commit v4 on v3

--- a/solution.py
+++ b/solution.py
@@ -100,14 +100,14 @@
 
 
 def build_marks(packed_ref, corners_ref, cols_ref, marks_ref, lanes_ref, slots_ref):
-    node_iota = lax.broadcasted_iota(jnp.int32, (64, 128), 0)
+    node_iota = lax.broadcasted_iota(jnp.int32, (32, 128), 0)
     lane_iota = lax.broadcasted_iota(jnp.int32, (128, 128), 0)
 
     def corner_marks(g, carry):
         for i in range(4):
             block = g * 4 + i
             for c in range(4):
-                ids = corners_ref[pl.ds(block * 4 + c, 1), :]
+                ids = corners_ref[pl.ds(block * 4 + c, 1), :] & 31
                 marks_ref[block, :, c * 128 : (c + 1) * 128] = mark(node_iota == ids)
         return carry
 
@@ -167,15 +167,20 @@
                 spread_ref[start + 48 : start + 56, :] = low_piece(grads[c][r])
 
 
-def block_sums(j, spread_ref, marks_ref, pairs_ref):
+def block_sums(j, spread_ref, corners_ref, marks_ref, pairs_ref):
     found = []
     for i in range(8):
         sums = []
         for half in range(2):
-            rows = [
-                spread_ref[pl.ds(c * 96 + half * 8 + i, 8, stride=16), :].astype(jnp.bfloat16) for c in range(4)
-            ]
-            sums.append(nt_dot(jnp.concatenate(rows, axis=1), marks_ref[half * 64 + j * 8 + i]))
+            block = half * 64 + j * 8 + i
+            parts = []
+            for c in range(4):
+                rows = spread_ref[pl.ds(c * 96 + half * 8 + i, 8, stride=16), :]
+                upper = jnp.broadcast_to(corners_ref[pl.ds(block * 4 + c, 1), :], (8, 128)) >= 32
+                split = [jnp.where(upper, 0.0, rows), jnp.where(upper, rows, 0.0)]
+                parts.append(jnp.concatenate(split, axis=0).astype(jnp.bfloat16))
+            out = nt_dot(jnp.concatenate(parts, axis=1), marks_ref[block])
+            sums += [out[0:8, :], out[8:16, :]]
         both = jnp.concatenate(sums, axis=1)
         pair = both[0:3, :] + both[3:6, :]
         pairs_ref[j * 8 + i, 0:3, :] = pair
@@ -198,22 +203,19 @@
 
 
 def ghost_rows(ghost_ref, packed_ref, part_ref, corners_ref, spreads, marks_ref, lanes_ref, pairs_ref, acc_ref):
-    even_ref, odd_ref = spreads
     tets = functools.partial(tet_spread, ghost_ref=ghost_ref, packed_ref=packed_ref, part_ref=part_ref)
 
-    def body(g, carry):
-        pairs = block_sums(2 * g, even_ref, marks_ref, pairs_ref)
-        tets(2 * g + 1, corners_ref=corners_ref, spread_ref=odd_ref)
-        first = row_group(2 * g, pairs, packed_ref, lanes_ref, OWN_ROWS, GPAD)
-        pairs = block_sums(2 * g + 1, odd_ref, marks_ref, pairs_ref)
-        tets(jnp.minimum(2 * g + 2, 7), corners_ref=corners_ref, spread_ref=even_ref)
-        second = row_group(2 * g + 1, pairs, packed_ref, lanes_ref, OWN_ROWS, GPAD)
-        acc_ref[...] += first + second
-        return carry
-
     acc_ref[...] = jnp.zeros_like(acc_ref)
-    tets(0, corners_ref=corners_ref, spread_ref=even_ref)
-    lax.fori_loop(0, 4, body, 0)
+    tets(0, corners_ref=corners_ref, spread_ref=spreads[0])
+    before = None
+    for j in range(8):
+        pairs = block_sums(j, spreads[j % 2], corners_ref, marks_ref, pairs_ref)
+        if j < 7:
+            tets(j + 1, corners_ref=corners_ref, spread_ref=spreads[(j + 1) % 2])
+        if j > 0:
+            acc_ref[...] += row_group(j - 1, before, packed_ref, lanes_ref, OWN_ROWS, GPAD)
+        before = pairs
+    acc_ref[...] += row_group(7, before, packed_ref, lanes_ref, OWN_ROWS, GPAD)
 
 
 def own_rows(packed_ref, pairs_ref, lanes_ref, acc_ref):
@@ -331,6 +333,7 @@
     pairs_ref,
     ghost_acc,
     own_acc,
+    shift_ref,
     load_sem,
     send_sem,
     recv_sem,
@@ -391,12 +394,17 @@
         for copy in copies:
             copy.wait_recv()
         grad = own + returned_gradient(back_ref.at[step], cols_ref, slots_ref)
-        value = pos_ref[...] - jnp.concatenate([free, free, free], axis=0) * grad
+        shift = jnp.concatenate([free, free, free], axis=0) * grad
+        if step > 0:
+            total = shift_ref[...] + shift
+        else:
+            total = shift
         if step < ITERS - 1:
-            pos_ref[...] = value
+            shift_ref[...] = total
+            pos_ref[...] = pos_ref[...] - shift
             gather_payload(pos_ref, cols_ref, pay_ref.at[step + 1])
         else:
-            store_positions(value, done_ref)
+            store_positions(total, done_ref)
     for copy in started:
         copy.wait_send()
 
@@ -411,7 +419,7 @@
     counts = send_count.transpose(0, 1, 3, 2)
     inputs = (positions, mask, send_list, counts, block_nodes, corners)
     slots = pltpu.VMEM((ITERS, NPAIR, 4, 128), jnp.float32)
-    return pl.pallas_call(
+    moved = pl.pallas_call(
         smooth_kernel,
         out_shape=jax.ShapeDtypeStruct((3, 2048), jnp.float32),
         in_specs=[ANY] * 6,
@@ -428,12 +436,13 @@
             pltpu.VMEM((3, 64, 128), jnp.float32),
             pltpu.VMEM((26 * 16, 128), jnp.float32),
             pltpu.VMEM((26 * 16, 128), jnp.float32),
-            pltpu.VMEM((128, 64, 512), jnp.bfloat16),
+            pltpu.VMEM((128, 32, 512), jnp.bfloat16),
             pltpu.VMEM((8, 128, 1024), jnp.bfloat16),
             pltpu.VMEM((128, NPAIR * 128), jnp.bfloat16),
             pltpu.VMEM((64, 8, 128), jnp.float32),
             pltpu.VMEM((6 * GPAD, 128), jnp.float32),
             pltpu.VMEM((6 * OWN_ROWS, 128), jnp.float32),
+            pltpu.VMEM((48, 128), jnp.float32),
             pltpu.SemaphoreType.DMA((6,)),
             pltpu.SemaphoreType.DMA((2 * ITERS, NPAIR)),
             pltpu.SemaphoreType.DMA((2 * ITERS, NPAIR)),
@@ -441,6 +450,7 @@
         compiler_params=pltpu.CompilerParams(collective_id=0, has_side_effects=True),
         name="smooth",
     )(*inputs)
+    return positions - moved
 
 
 def solution(mesh):

time: 51.1 us -> 47.8 us (0.935)
  Pallas kernels: 49.5 us -> 46.2 us
  other arithmetic: 0 us -> 1.38 us
  local copies, waits for them, and re-layouts: 1.38 us -> 0.01 us
    pallas_call x1, Pallas kernels: 49.5 us -> 46.2 us  [per_device(): pl.pallas_call(smooth_kernel, out_shape=jax.ShapeDtypeStruct((3, 2048), j...]
    sub x0 -> x1, other arithmetic: none -> 1.38 us  [per_device(): return positions - moved]
    unnamed x1 -> x2, local copies, waits for them, and re-layouts: 1.38 us -> 0.01 us
where the time goes in v4:
time: 47.8 us; the launch traced here: 47.6 us
  Pallas kernels  46.2 us (97%)
  other arithmetic  1.38 us (3%)
    pallas_call x1, Pallas kernels, per_device(): pl.pallas_call(smooth_kernel, out_shape=jax.ShapeDtypeStruct((3, 2048), j...  46.2 us
    sub x1, other arithmetic, per_device(): return positions - moved  1.38 us

profile of v4, /device:TPU:1, one launch (start us, length us, event | category | flops | bytes accessed | tf_op | source)
XLA Modules:
  0.0 47.6 jit_solution(5855109251019324155)
XLA Ops:
  0.0 0.0 copy-start
  0.0 46.2 %smooth.1 = f32[3,2048]{1,0:T(4,128)} custom-call(f32[3,2048]{1,0:T(4,128)} %raw_hbm.1, s32[16,128]{1,0:T(8,128)} %bitcast.8, s32[1,1,5,4,128]{4,3,2,1,0:T(4,128)} %list_hbm.1, s32[1,1,4,5]{3,2,1,0:T(4,128)} %bitcast.9, s32[64,128]{1,0:T(8,128)} %nodes_hbm.1, s32[512,128]{1,0:T(8,128)} %bitcast.7), custom_call_target="tpu_custom_call" | custom-call | tf_op jit(solution)/shard_map/smooth/pallas_call | solution.py:422
  46.2 0.0 copy-done
  46.2 1.4 %sub.3 = f32[3,2048]{1,0:T(4,128)} subtract(f32[3,2048]{1,0:T(4,128)S(1)} %copy-done, f32[3,2048]{1,0:T(4,128)} %smooth.1) | non-fusion elementwise | flops 6144 | bytes 73728 | tf_op jit(solution)/shard_map/sub | solution.py:453
Async XLA Ops:
  0.0 46.2 %copy-start = (f32[3,2048]{1,0:T(4,128)S(1)}, f32[3,2048]{1,0:T(4,128)}, u32[]{:S(2)}) copy-start(f32[3,2048]{1,0:T(4,128)} %raw_hbm.1) | copy-start | bytes 73732

commit v5 on v4

--- a/solution.py
+++ b/solution.py
@@ -121,7 +121,7 @@
 
     lax.fori_loop(0, 8, lane_marks, 0)
     for n in range(NPAIR):
-        slots_ref[:, n * 128 : (n + 1) * 128] = mark(lane_iota == (cols_ref[n : n + 1, :] & 127))
+        slots_ref[n] = mark(lane_iota == (cols_ref[n : n + 1, :] & 127))
 
 
 def gather_own(pos_ref, packed_ref, part_ref):
@@ -142,7 +142,24 @@
     lax.fori_loop(0, GROUPS, body, 0)
 
 
-def tet_spread(j, ghost_ref, packed_ref, part_ref, corners_ref, spread_ref):
+def gather_near(ghost_ref, packed_ref, part_ref, taken):
+    def body(g, carry):
+        for i in range(2):
+            rows = pl.ds(pl.multiple_of(g * 16 + i * 8, 8), 8)
+            cols = packed_ref[rows, :]
+            high = cols >> 7
+            low = cols & 127
+            for r in range(3):
+                picked = part_ref[r, rows, :]
+                for n in taken:
+                    picked = jnp.where(high == OWN_ROWS + n, lane_take(ghost_ref[n, r : r + 1, :], low), picked)
+                part_ref[r, rows, :] = picked
+        return carry
+
+    lax.fori_loop(0, GROUPS, body, 0)
+
+
+def tet_spread(j, taken, ghost_ref, packed_ref, part_ref, corners_ref, spread_ref):
     base = pl.multiple_of(j * 8, 8)
     cols = packed_ref[pl.ds(base, 8), :]
     high = cols >> 7
@@ -150,7 +167,7 @@
     source = []
     for r in range(3):
         picked = part_ref[r, pl.ds(base, 8), :]
-        for n in range(NPAIR):
+        for n in taken:
             picked = jnp.where(high == OWN_ROWS + n, lane_take(ghost_ref[n, r : r + 1, :], low), picked)
         source.append(picked)
     for half in range(2):
@@ -202,8 +219,8 @@
     return nt_dot(jnp.concatenate(left, axis=1), lanes_ref[j])
 
 
-def ghost_rows(ghost_ref, packed_ref, part_ref, corners_ref, spreads, marks_ref, lanes_ref, pairs_ref, acc_ref):
-    tets = functools.partial(tet_spread, ghost_ref=ghost_ref, packed_ref=packed_ref, part_ref=part_ref)
+def ghost_rows(taken, ghost_ref, packed_ref, part_ref, corners_ref, spreads, marks_ref, lanes_ref, pairs_ref, acc_ref):
+    tets = functools.partial(tet_spread, taken=taken, ghost_ref=ghost_ref, packed_ref=packed_ref, part_ref=part_ref)
 
     acc_ref[...] = jnp.zeros_like(acc_ref)
     tets(0, corners_ref=corners_ref, spread_ref=spreads[0])
@@ -239,18 +256,20 @@
             out_ref[n, r : r + 1, :] = both[n : n + 1, :]
 
 
-def returned_gradient(back_ref, cols_ref, slots_ref):
+def returned_gradient(back_ref, cols_ref, slots_ref, taken):
     high_iota = lax.broadcasted_iota(jnp.int32, (OWN_ROWS, 128), 0)
     left_parts = []
-    for n in range(NPAIR):
-        cols = cols_ref[n : n + 1, :]
+    right_parts = []
+    for n in taken:
+        cols = cols_ref[pl.ds(n, 1), :]
         chosen = high_iota == (cols >> 7)
         values = jnp.where(cols >= 0, back_ref[n, 0:3, :], 0.0)
         rest = low_piece(values)
         stack = [jnp.where(chosen, values[r : r + 1, :], 0.0) for r in range(3)]
         stack += [jnp.where(chosen, rest[r : r + 1, :], 0.0) for r in range(3)]
         left_parts.append(jnp.concatenate(stack, axis=0).astype(jnp.bfloat16))
-    out = nt_dot(jnp.concatenate(left_parts, axis=1), slots_ref[...])
+        right_parts.append(slots_ref[n])
+    out = nt_dot(jnp.concatenate(left_parts, axis=1), jnp.concatenate(right_parts, axis=1))
     return out[0:48, :] + out[48:96, :]
 
 
@@ -362,6 +381,9 @@
     for load in loads[3:6]:
         load.wait()
     pl.semaphore_wait(barrier, len(ahead))
+    sub = lax.axis_index("sub")
+    far = [k * SUBS + lax.rem(sub + 2, SUBS) for k in range(SLOTS)]
+    near = [k * SUBS + lax.rem(sub + turn, SUBS) for k in range(SLOTS) for turn in (0, 1, 3)]
     started = []
     for step in range(ITERS):
         copies = exchange(ahead, pay_ref.at[step], ghost_ref.at[step], send_sem.at[2 * step], recv_sem.at[2 * step])
@@ -370,9 +392,15 @@
             prepare_blocks(nodes_ref, packed_ref)
             build_marks(packed_ref, corners_ref, cols_ref, marks_ref, lanes_ref, slots_ref)
         gather_own(pos_ref, packed_ref, part_ref)
-        for copy in copies:
-            copy.wait_recv()
+        for copy, partner in zip(copies, ahead):
+            if partner[1] != 2:
+                copy.wait_recv()
+        gather_near(ghost_ref.at[step], packed_ref, part_ref, near)
+        for copy, partner in zip(copies, ahead):
+            if partner[1] == 2:
+                copy.wait_recv()
         ghost_rows(
+            far,
             ghost_ref.at[step],
             packed_ref,
             part_ref,
@@ -391,9 +419,14 @@
         own_rows(packed_ref, pairs_ref, lanes_ref, own_acc)
         own = own_acc[0:48, :] + own_acc[48:96, :]
         free = jnp.where(mask_ref[...] == 0, STEP, 0.0)
-        for copy in copies:
-            copy.wait_recv()
-        grad = own + returned_gradient(back_ref.at[step], cols_ref, slots_ref)
+        for copy, partner in zip(copies, behind):
+            if partner[1] != 2:
+                copy.wait_recv()
+        own = own + returned_gradient(back_ref.at[step], cols_ref, slots_ref, near)
+        for copy, partner in zip(copies, behind):
+            if partner[1] == 2:
+                copy.wait_recv()
+        grad = own + returned_gradient(back_ref.at[step], cols_ref, slots_ref, far)
         shift = jnp.concatenate([free, free, free], axis=0) * grad
         if step > 0:
             total = shift_ref[...] + shift
@@ -438,7 +471,7 @@
             pltpu.VMEM((26 * 16, 128), jnp.float32),
             pltpu.VMEM((128, 32, 512), jnp.bfloat16),
             pltpu.VMEM((8, 128, 1024), jnp.bfloat16),
-            pltpu.VMEM((128, NPAIR * 128), jnp.bfloat16),
+            pltpu.VMEM((NPAIR, 128, 128), jnp.bfloat16),
             pltpu.VMEM((64, 8, 128), jnp.float32),
             pltpu.VMEM((6 * GPAD, 128), jnp.float32),
             pltpu.VMEM((6 * OWN_ROWS, 128), jnp.float32),

time: 47.8 us -> 49.3 us (1.031)
  Pallas kernels: 46.2 us -> 47.6 us
    pallas_call x1, Pallas kernels: 46.2 us -> 47.6 us  [per_device(): pl.pallas_call(smooth_kernel, out_shape=jax.ShapeDtypeStruct((3, 2048), j...]
where the time goes in v5:
time: 49.3 us; the launch traced here: 49 us
  Pallas kernels  47.6 us (97%)
  other arithmetic  1.38 us (3%)
    pallas_call x1, Pallas kernels, per_device(): pl.pallas_call(smooth_kernel, out_shape=jax.ShapeDtypeStruct((3, 2048), j...  47.6 us
    sub x1, other arithmetic, per_device(): return positions - moved  1.38 us

profile of v5, /device:TPU:1, one launch (start us, length us, event | category | flops | bytes accessed | tf_op | source)
XLA Modules:
  0.0 49.0 jit_solution(4006350626075587006)
XLA Ops:
  0.0 0.0 copy-start
  0.0 47.6 %smooth.1 = f32[3,2048]{1,0:T(4,128)} custom-call(f32[3,2048]{1,0:T(4,128)} %raw_hbm.1, s32[16,128]{1,0:T(8,128)} %bitcast.8, s32[1,1,5,4,128]{4,3,2,1,0:T(4,128)} %list_hbm.1, s32[1,1,4,5]{3,2,1,0:T(4,128)} %bitcast.9, s32[64,128]{1,0:T(8,128)} %nodes_hbm.1, s32[512,128]{1,0:T(8,128)} %bitcast.7), custom_call_target="tpu_custom_call" | custom-call | tf_op jit(solution)/shard_map/smooth/pallas_call | solution.py:455
  47.6 0.0 copy-done
  47.6 1.4 %sub.3 = f32[3,2048]{1,0:T(4,128)} subtract(f32[3,2048]{1,0:T(4,128)S(1)} %copy-done, f32[3,2048]{1,0:T(4,128)} %smooth.1) | non-fusion elementwise | flops 6144 | bytes 73728 | tf_op jit(solution)/shard_map/sub | solution.py:486
Async XLA Ops:
  0.0 47.6 %copy-start = (f32[3,2048]{1,0:T(4,128)S(1)}, f32[3,2048]{1,0:T(4,128)}, u32[]{:S(2)}) copy-start(f32[3,2048]{1,0:T(4,128)} %raw_hbm.1) | copy-start | bytes 73732
